TPU v7x, 32 devices: a whole 2x2x4 slice. The times are simulated.
32 devices in a mesh: views: 2 (over x), depth: 2 (over core), lat: 8 (over z, y).
Axes of the slice: x: 2, y: 2, z: 4, core: 2. Of those that a mesh axis runs over, the one named last changes fastest.
Arguments:
- volume: bfloat16 [256, 128, 2048], P(('views', 'depth'), 'lat'), parts along dimension 0, may hold values from -6 to 6
- shift_table: int32 [256], P('views'), parts along dimension 0, may hold values from 0 to 48, as said below
- slab_order: int32 [16, 2], P(('views', 'lat')), parts along dimension 0, may hold values from 0 to 1, each once within a row
- centers: float32 [8], replicated, may hold values from -2 to 2
- widths: float32 [8], replicated, may hold values from 0.5 to 4
- extinct: float32 [8], replicated, may hold values from 0.2 to 3
- colors: float32 [3, 8], replicated, may hold values from 0 to 1
Outputs:
- image: float32 [4, 256, 2048], P(None, ('views', 'lat'), 'depth'), parts along dimension 1
There are 2 independent parts, one for each index of `views`. A program takes and returns all parts, laid end to end along the dimension named above; an argument that names none is the same for every part. Nothing has to cross between parts.
Inputs may be any that keep to these rules, and one draw needn't show every extreme that they name: `shift_table`: every slice's shift lies in 0 to 48; some slice has shift 0 and some slice has shift exactly 48. `slab_order`: each row is a permutation of the slab indices; its entry 0 is the slab nearest the eye for that band of rows.
All inputs are finite; a program needn't handle non-finite values.
Results may differ from a plain program's by a relative error of at most 0.0003.
Values may be sent and summed in bfloat16 or wider, within the bound.
No kernel may reach another device: no remote copies, remote signals or barrier semaphores. Data moves between devices by JAX's collectives and lax.ppermute only.
A program may use at most 128 MiB of HBM per device.

v0:
```python
import jax
import jax.numpy as jnp
from jax import lax
from jax.sharding import PartitionSpec as P


def from_behind(block, axis, distance):
    devices = range(lax.axis_size(axis))
    route = [(i - distance, i) for i in devices if i - distance in devices]
    return lax.ppermute(block, axis, route)


def classify(samples, centers, widths, extinct, colors, inv_depth):
    optical = jnp.zeros(samples.shape, jnp.float32)
    emission = jnp.zeros((3,) + samples.shape, jnp.float32)
    for lobe_index in range(centers.shape[0]):
        lobe_value = jnp.exp(-jnp.square(samples - centers[lobe_index]) * widths[lobe_index])
        optical = optical + extinct[lobe_index] * lobe_value
        emission = (
            emission + colors[:, lobe_index].reshape((3,) + (1,) * samples.ndim) * lobe_value[None]
        )
    return (optical * inv_depth, emission)


def take_rows(plane, offset, row_count):
    return lax.dynamic_slice_in_dim(plane, offset, row_count, 0)


def local(volume, shift_table, slab_order, centers, widths, extinct, colors):
    slab_count = lax.axis_size("depth")
    slice_count, row_count, col_count = volume.shape
    slab_start = lax.axis_index("depth") * slice_count
    local_shift = lax.dynamic_slice_in_dim(shift_table, slab_start, slice_count)
    brick_steps = local_shift // row_count
    offsets = local_shift - brick_steps * row_count
    high_bit = (brick_steps // 2 % 2 == 1)[:, None, None]
    low_bit = (brick_steps % 2 == 1)[:, None, None]
    farther = from_behind(volume, "lat", -2)
    held = jnp.where(high_bit, farther, volume)
    nearer = from_behind(held, "lat", -1)
    held = jnp.where(low_bit, nearer, held)
    after = from_behind(held, "lat", -1)
    extended = jnp.concatenate([held, after], axis=1)
    forward = slab_order[0, 0] == 0
    inv_depth = 1.0 / (slice_count * slab_count)
    block_size = 8
    block_count = slice_count // block_size

    def advance(running, counter):
        depth_sum, color = running
        block_index = jnp.where(forward, counter, block_count - 1 - counter)
        block_start = block_index * block_size
        block_cells = lax.dynamic_slice_in_dim(extended, block_start, block_size, 0)
        shifts = lax.dynamic_slice_in_dim(offsets, block_start, block_size)
        samples = jax.vmap(take_rows, in_axes=(0, 0, None))(block_cells, shifts, row_count).astype(
            jnp.float32
        )
        optical, emission = classify(samples, centers, widths, extinct, colors, inv_depth)
        inclusive = jnp.cumsum(optical, axis=0)
        block_total = inclusive[-1]
        before = jnp.where(forward, inclusive - optical, block_total[None] - inclusive)
        weight = jnp.exp(-(depth_sum[None] + before)) * (1.0 - jnp.exp(-optical))
        color = color + jnp.sum(weight[None] * emission, axis=1)
        return ((depth_sum + block_total, color), None)

    start = (
        jnp.zeros((row_count, col_count), jnp.float32),
        jnp.zeros((3, row_count, col_count), jnp.float32),
    )
    (depth_sum, color), _ = lax.scan(advance, start, jnp.arange(block_count, dtype=jnp.int32))
    partial_value = jnp.concatenate([color, depth_sum[None]], axis=0)
    traded = lax.all_to_all(partial_value, "depth", split_axis=2, concat_axis=0, tiled=True)
    front_image = jnp.where(forward, traded[:4], traded[4:])
    back_image = jnp.where(forward, traded[4:], traded[:4])
    rgb_part = front_image[:3] + jnp.exp(-front_image[3])[None] * back_image[:3]
    opacity = 1.0 - jnp.exp(-(front_image[3] + back_image[3]))
    return jnp.concatenate([rgb_part, opacity[None]], axis=0)


def solution(mesh):
    in_specs = (
        P(("views", "depth"), "lat", None),
        P("views"),
        P(("views", "lat"), None),
        P(),
        P(),
        P(),
        P(),
    )
    out_specs = P(None, ("views", "lat"), "depth")
    return jax.shard_map(local, mesh=mesh, in_specs=in_specs, out_specs=out_specs, check_vma=False)
```

profile of v0, /device:TPU:0, one launch (start us, length us, event | category | flops | bytes accessed | tf_op | source)
XLA Modules:
  0.0 852.3 jit_solution(10103599735082312356)
XLA Ops:
  7.9 94.4 %collective-permute-done = bf16[64,16,2048]{2,0,1:T(8,128)(2,1)} collective-permute-done((bf16[64,16,2048]{2,0,1:T(8,128)(2,1)}, bf16[64,16,2048]{2,0,1:T(8,128)(2,1)}, u32[]{:S(2)}, u32[]{:S(2)}) %collective-permute-start) | collective-permute-done | bytes 4194336 | tf_op jit(solution)/shard_map/ppermute | solution.py:10
  111.6 92.3 %collective-permute-done.1 = bf16[64,16,2048]{2,0,1:T(8,128)(2,1)S(1)} collective-permute-done((bf16[64,16,2048]{2,0,1:T(8,128)(2,1)S(1)}, bf16[64,16,2048]{2,0,1:T(8,128)(2,1)S(1)}, u32[]{:S(2)}, u32[]{:S(2)}) %collective-permute-start.1) | collective-permute-done | bytes 4194336 | tf_op jit(solution)/shard_map/ppermute | solution.py:10
  207.9 91.9 %collective-permute-done.2 = bf16[64,16,2048]{2,0,1:T(8,128)(2,1)} collective-permute-done((bf16[64,16,2048]{2,0,1:T(8,128)(2,1)}, bf16[64,16,2048]{2,0,1:T(8,128)(2,1)}, u32[]{:S(2)}, u32[]{:S(2)}) %collective-permute-start.2) | collective-permute-done | bytes 4194336 | tf_op jit(solution)/shard_map/ppermute | solution.py:10
  307.2 520.3 %while.13 = (s32[]{:T(128)}, f32[16,2048]{1,0:T(8,128)S(1)}, f32[3,16,2048]{2,1,0:T(8,128)S(1)}, f32[8]{0:T(128)S(1)}, s32[8]{0:T(128)S(1)}, /*index=5*/pred[]{:...) while((s32[]{:T(128)}, f32[16,2048]{1,0:T(8,128)S(1)}, ...), condition=%wide.region_3.4_spmd.clone, body=%wide.region_0.3_spmd.clone.sunk | while | flops 51806280 | bytes 49546372 | solution.py:70
  314.2 16.9 %add_multiply_fusion.2 = f32[8,16,2048]{2,0,1:T(8,128)S(1)} fusion(f32[]{:T(128)} %bitcast.108, f32[]{:T(128)} %bitcast.109, f32[]{:T(128)} %bitcast.110, f32[]{:T(128)} %bitcast.111, f32[]{:T(128)} %bitcast.112, f32[]{:T(128)} %bitcast.113, f32[]{:T(128)} %bitcast.114, f32[]{:T(128)} %bitcast.115, f32[]{:T(128)} %bitcast.116, f32[]{:T(128)} %bitcast.117, ...), kind=kLoop, calls=%fused_computation.43.clone.2 | loop fusion | flops 12845056 | bytes 1572960 | tf_op jit(solution)/shard_map/while/body/eval_jaxpr/mul | solution.py:22
  336.0 17.4 %subtract_multiply_fusion.2 = f32[8,16,2048]{2,0,1:T(8,128)S(1)} fusion(f32[8,16,2048]{2,0,1:T(8,128)S(1)} %reduce_window_sum.13, f32[16,2048]{1,0:T(8,128)S(1)} %bitcast.137, f32[16,2048]{1,0:T(8,128)S(1)} %get-tuple-element.386, pred[]{:T(512)} %get-tuple-element.426, f32[]{:T(128)} %bitcast.116, f32[]{:T(128)} %bitcast.117, f32[]{:T(128)} %bitcast.108, ...), kind=kLoop, calls=%fused_computation.42.clone.1 | loop fusion | flops 14942208 | bytes 2883681 | tf_op jit(solution)/shard_map/while/body/eval_jaxpr/mul | solution.py:62
  354.0 11.4 %fusion.56 = (f32[8,16,2048]{2,0,1:T(8,128)S(1)}, f32[8,16,2048]{2,0,1:T(8,128)S(1)}, f32[8,16,2048]{2,0,1:T(8,128)S(1)}, f32[8,16,2048]{2,0,1:T(8,128)S(1)}, f3...) fusion(bf16[8,16,2048]{2,0,1:T(8,128)(2,1)S(1)} %gather_fusion,, ...), kind=kLoop, calls=%fused_computation.13.clone.2 | loop fusion | flops 8650752 | bytes 8912960 | tf_op jit(solution)/shard_map/while/body/eval_jaxpr/exp | solution.py:17
  379.1 16.9 %add_multiply_fusion.2 = f32[8,16,2048]{2,0,1:T(8,128)S(1)} fusion(f32[]{:T(128)} %bitcast.108, f32[]{:T(128)} %bitcast.109, f32[]{:T(128)} %bitcast.110, f32[]{:T(128)} %bitcast.111, f32[]{:T(128)} %bitcast.112, f32[]{:T(128)} %bitcast.113, f32[]{:T(128)} %bitcast.114, f32[]{:T(128)} %bitcast.115, f32[]{:T(128)} %bitcast.116, f32[]{:T(128)} %bitcast.117, ...), kind=kLoop, calls=%fused_computation.43.clone.2 | loop fusion | flops 12845056 | bytes 1572960 | tf_op jit(solution)/shard_map/while/body/eval_jaxpr/mul | solution.py:22
  401.0 17.4 %subtract_multiply_fusion.2 = f32[8,16,2048]{2,0,1:T(8,128)S(1)} fusion(f32[8,16,2048]{2,0,1:T(8,128)S(1)} %reduce_window_sum.13, f32[16,2048]{1,0:T(8,128)S(1)} %bitcast.137, f32[16,2048]{1,0:T(8,128)S(1)} %get-tuple-element.386, pred[]{:T(512)} %get-tuple-element.426, f32[]{:T(128)} %bitcast.116, f32[]{:T(128)} %bitcast.117, f32[]{:T(128)} %bitcast.108, ...), kind=kLoop, calls=%fused_computation.42.clone.1 | loop fusion | flops 14942208 | bytes 2883681 | tf_op jit(solution)/shard_map/while/body/eval_jaxpr/mul | solution.py:62
  419.0 11.4 %fusion.56 = (f32[8,16,2048]{2,0,1:T(8,128)S(1)}, f32[8,16,2048]{2,0,1:T(8,128)S(1)}, f32[8,16,2048]{2,0,1:T(8,128)S(1)}, f32[8,16,2048]{2,0,1:T(8,128)S(1)}, f3...) fusion(bf16[8,16,2048]{2,0,1:T(8,128)(2,1)S(1)} %gather_fusion,, ...), kind=kLoop, calls=%fused_computation.13.clone.2 | loop fusion | flops 8650752 | bytes 8912960 | tf_op jit(solution)/shard_map/while/body/eval_jaxpr/exp | solution.py:17
  444.1 16.9 %add_multiply_fusion.2 = f32[8,16,2048]{2,0,1:T(8,128)S(1)} fusion(f32[]{:T(128)} %bitcast.108, f32[]{:T(128)} %bitcast.109, f32[]{:T(128)} %bitcast.110, f32[]{:T(128)} %bitcast.111, f32[]{:T(128)} %bitcast.112, f32[]{:T(128)} %bitcast.113, f32[]{:T(128)} %bitcast.114, f32[]{:T(128)} %bitcast.115, f32[]{:T(128)} %bitcast.116, f32[]{:T(128)} %bitcast.117, ...), kind=kLoop, calls=%fused_computation.43.clone.2 | loop fusion | flops 12845056 | bytes 1572960 | tf_op jit(solution)/shard_map/while/body/eval_jaxpr/mul | solution.py:22
  466.0 17.4 %subtract_multiply_fusion.2 = f32[8,16,2048]{2,0,1:T(8,128)S(1)} fusion(f32[8,16,2048]{2,0,1:T(8,128)S(1)} %reduce_window_sum.13, f32[16,2048]{1,0:T(8,128)S(1)} %bitcast.137, f32[16,2048]{1,0:T(8,128)S(1)} %get-tuple-element.386, pred[]{:T(512)} %get-tuple-element.426, f32[]{:T(128)} %bitcast.116, f32[]{:T(128)} %bitcast.117, f32[]{:T(128)} %bitcast.108, ...), kind=kLoop, calls=%fused_computation.42.clone.1 | loop fusion | flops 14942208 | bytes 2883681 | tf_op jit(solution)/shard_map/while/body/eval_jaxpr/mul | solution.py:62
  509.1 16.9 %add_multiply_fusion.2 = f32[8,16,2048]{2,0,1:T(8,128)S(1)} fusion(f32[]{:T(128)} %bitcast.108, f32[]{:T(128)} %bitcast.109, f32[]{:T(128)} %bitcast.110, f32[]{:T(128)} %bitcast.111, f32[]{:T(128)} %bitcast.112, f32[]{:T(128)} %bitcast.113, f32[]{:T(128)} %bitcast.114, f32[]{:T(128)} %bitcast.115, f32[]{:T(128)} %bitcast.116, f32[]{:T(128)} %bitcast.117, ...), kind=kLoop, calls=%fused_computation.43.clone.2 | loop fusion | flops 12845056 | bytes 1572960 | tf_op jit(solution)/shard_map/while/body/eval_jaxpr/mul | solution.py:22
  531.0 17.4 %subtract_multiply_fusion.2 = f32[8,16,2048]{2,0,1:T(8,128)S(1)} fusion(f32[8,16,2048]{2,0,1:T(8,128)S(1)} %reduce_window_sum.13, f32[16,2048]{1,0:T(8,128)S(1)} %bitcast.137, f32[16,2048]{1,0:T(8,128)S(1)} %get-tuple-element.386, pred[]{:T(512)} %get-tuple-element.426, f32[]{:T(128)} %bitcast.116, f32[]{:T(128)} %bitcast.117, f32[]{:T(128)} %bitcast.108, ...), kind=kLoop, calls=%fused_computation.42.clone.1 | loop fusion | flops 14942208 | bytes 2883681 | tf_op jit(solution)/shard_map/while/body/eval_jaxpr/mul | solution.py:62
  549.0 11.4 %fusion.56 = (f32[8,16,2048]{2,0,1:T(8,128)S(1)}, f32[8,16,2048]{2,0,1:T(8,128)S(1)}, f32[8,16,2048]{2,0,1:T(8,128)S(1)}, f32[8,16,2048]{2,0,1:T(8,128)S(1)}, f3...) fusion(bf16[8,16,2048]{2,0,1:T(8,128)(2,1)S(1)} %gather_fusion,, ...), kind=kLoop, calls=%fused_computation.13.clone.2 | loop fusion | flops 8650752 | bytes 8912960 | tf_op jit(solution)/shard_map/while/body/eval_jaxpr/exp | solution.py:17
  574.1 16.9 %add_multiply_fusion.2 = f32[8,16,2048]{2,0,1:T(8,128)S(1)} fusion(f32[]{:T(128)} %bitcast.108, f32[]{:T(128)} %bitcast.109, f32[]{:T(128)} %bitcast.110, f32[]{:T(128)} %bitcast.111, f32[]{:T(128)} %bitcast.112, f32[]{:T(128)} %bitcast.113, f32[]{:T(128)} %bitcast.114, f32[]{:T(128)} %bitcast.115, f32[]{:T(128)} %bitcast.116, f32[]{:T(128)} %bitcast.117, ...), kind=kLoop, calls=%fused_computation.43.clone.2 | loop fusion | flops 12845056 | bytes 1572960 | tf_op jit(solution)/shard_map/while/body/eval_jaxpr/mul | solution.py:22
  595.9 17.4 %subtract_multiply_fusion.2 = f32[8,16,2048]{2,0,1:T(8,128)S(1)} fusion(f32[8,16,2048]{2,0,1:T(8,128)S(1)} %reduce_window_sum.13, f32[16,2048]{1,0:T(8,128)S(1)} %bitcast.137, f32[16,2048]{1,0:T(8,128)S(1)} %get-tuple-element.386, pred[]{:T(512)} %get-tuple-element.426, f32[]{:T(128)} %bitcast.116, f32[]{:T(128)} %bitcast.117, f32[]{:T(128)} %bitcast.108, ...), kind=kLoop, calls=%fused_computation.42.clone.1 | loop fusion | flops 14942208 | bytes 2883681 | tf_op jit(solution)/shard_map/while/body/eval_jaxpr/mul | solution.py:62
  639.1 16.9 %add_multiply_fusion.2 = f32[8,16,2048]{2,0,1:T(8,128)S(1)} fusion(f32[]{:T(128)} %bitcast.108, f32[]{:T(128)} %bitcast.109, f32[]{:T(128)} %bitcast.110, f32[]{:T(128)} %bitcast.111, f32[]{:T(128)} %bitcast.112, f32[]{:T(128)} %bitcast.113, f32[]{:T(128)} %bitcast.114, f32[]{:T(128)} %bitcast.115, f32[]{:T(128)} %bitcast.116, f32[]{:T(128)} %bitcast.117, ...), kind=kLoop, calls=%fused_computation.43.clone.2 | loop fusion | flops 12845056 | bytes 1572960 | tf_op jit(solution)/shard_map/while/body/eval_jaxpr/mul | solution.py:22
  660.9 17.4 %subtract_multiply_fusion.2 = f32[8,16,2048]{2,0,1:T(8,128)S(1)} fusion(f32[8,16,2048]{2,0,1:T(8,128)S(1)} %reduce_window_sum.13, f32[16,2048]{1,0:T(8,128)S(1)} %bitcast.137, f32[16,2048]{1,0:T(8,128)S(1)} %get-tuple-element.386, pred[]{:T(512)} %get-tuple-element.426, f32[]{:T(128)} %bitcast.116, f32[]{:T(128)} %bitcast.117, f32[]{:T(128)} %bitcast.108, ...), kind=kLoop, calls=%fused_computation.42.clone.1 | loop fusion | flops 14942208 | bytes 2883681 | tf_op jit(solution)/shard_map/while/body/eval_jaxpr/mul | solution.py:62
  704.0 16.9 %add_multiply_fusion.2 = f32[8,16,2048]{2,0,1:T(8,128)S(1)} fusion(f32[]{:T(128)} %bitcast.108, f32[]{:T(128)} %bitcast.109, f32[]{:T(128)} %bitcast.110, f32[]{:T(128)} %bitcast.111, f32[]{:T(128)} %bitcast.112, f32[]{:T(128)} %bitcast.113, f32[]{:T(128)} %bitcast.114, f32[]{:T(128)} %bitcast.115, f32[]{:T(128)} %bitcast.116, f32[]{:T(128)} %bitcast.117, ...), kind=kLoop, calls=%fused_computation.43.clone.2 | loop fusion | flops 12845056 | bytes 1572960 | tf_op jit(solution)/shard_map/while/body/eval_jaxpr/mul | solution.py:22
  725.9 17.4 %subtract_multiply_fusion.2 = f32[8,16,2048]{2,0,1:T(8,128)S(1)} fusion(f32[8,16,2048]{2,0,1:T(8,128)S(1)} %reduce_window_sum.13, f32[16,2048]{1,0:T(8,128)S(1)} %bitcast.137, f32[16,2048]{1,0:T(8,128)S(1)} %get-tuple-element.386, pred[]{:T(512)} %get-tuple-element.426, f32[]{:T(128)} %bitcast.116, f32[]{:T(128)} %bitcast.117, f32[]{:T(128)} %bitcast.108, ...), kind=kLoop, calls=%fused_computation.42.clone.1 | loop fusion | flops 14942208 | bytes 2883681 | tf_op jit(solution)/shard_map/while/body/eval_jaxpr/mul | solution.py:62
  743.9 11.4 %fusion.56 = (f32[8,16,2048]{2,0,1:T(8,128)S(1)}, f32[8,16,2048]{2,0,1:T(8,128)S(1)}, f32[8,16,2048]{2,0,1:T(8,128)S(1)}, f32[8,16,2048]{2,0,1:T(8,128)S(1)}, f3...) fusion(bf16[8,16,2048]{2,0,1:T(8,128)(2,1)S(1)} %gather_fusion,, ...), kind=kLoop, calls=%fused_computation.13.clone.2 | loop fusion | flops 8650752 | bytes 8912960 | tf_op jit(solution)/shard_map/while/body/eval_jaxpr/exp | solution.py:17
  769.0 16.9 %add_multiply_fusion.2 = f32[8,16,2048]{2,0,1:T(8,128)S(1)} fusion(f32[]{:T(128)} %bitcast.108, f32[]{:T(128)} %bitcast.109, f32[]{:T(128)} %bitcast.110, f32[]{:T(128)} %bitcast.111, f32[]{:T(128)} %bitcast.112, f32[]{:T(128)} %bitcast.113, f32[]{:T(128)} %bitcast.114, f32[]{:T(128)} %bitcast.115, f32[]{:T(128)} %bitcast.116, f32[]{:T(128)} %bitcast.117, ...), kind=kLoop, calls=%fused_computation.43.clone.2 | loop fusion | flops 12845056 | bytes 1572960 | tf_op jit(solution)/shard_map/while/body/eval_jaxpr/mul | solution.py:22
  790.9 17.4 %subtract_multiply_fusion.2 = f32[8,16,2048]{2,0,1:T(8,128)S(1)} fusion(f32[8,16,2048]{2,0,1:T(8,128)S(1)} %reduce_window_sum.13, f32[16,2048]{1,0:T(8,128)S(1)} %bitcast.137, f32[16,2048]{1,0:T(8,128)S(1)} %get-tuple-element.386, pred[]{:T(512)} %get-tuple-element.426, f32[]{:T(128)} %bitcast.116, f32[]{:T(128)} %bitcast.117, f32[]{:T(128)} %bitcast.108, ...), kind=kLoop, calls=%fused_computation.42.clone.1 | loop fusion | flops 14942208 | bytes 2883681 | tf_op jit(solution)/shard_map/while/body/eval_jaxpr/mul | solution.py:62
  (221 shorter events, 242.1 us)
Async XLA Ops:
  0.0 7.7 copy-start.4
  6.4 95.8 %collective-permute-start = (bf16[64,16,2048]{2,0,1:T(8,128)(2,1)}, bf16[64,16,2048]{2,0,1:T(8,128)(2,1)}, u32[]{:S(2)}, u32[]{:S(2)}) collective-permute-start(bf16[64,16,2048]{2,0,1:T(8,128)(2,1)} %copy.76), channel_id=1, source_target_pairs={{2,0},{3,1},{4,2},{5,3},{6,4},{7,5},{10,8},{11,9},{12,10},{13,11},... | collective-permute-start | bytes 12582920 | tf_op jit(solution)/shard_map/ppermute | solution.py:10
  110.3 93.6 %collective-permute-start.1 = (bf16[64,16,2048]{2,0,1:T(8,128)(2,1)S(1)}, bf16[64,16,2048]{2,0,1:T(8,128)(2,1)S(1)}, u32[]{:S(2)}, u32[]{:S(2)}) collective-permute-start(bf16[64,16,2048]{2,0,1:T(8,128)(2,1)S(1)} %broadcast_select_fusion.1), channel_id=1, source_target_pairs={{1,0},{2,1},{3,2},{4,3},{5,4},{6,5},{7,6},{9,8},{10,9},{11,10},{12... | collective-permute-start | bytes 12582920 | tf_op jit(solution)/shard_map/ppermute | solution.py:10
  204.0 3.8 copy-start.3
  204.0 3.9 copy-start.5
  206.4 93.4 %collective-permute-start.2 = (bf16[64,16,2048]{2,0,1:T(8,128)(2,1)}, bf16[64,16,2048]{2,0,1:T(8,128)(2,1)}, u32[]{:S(2)}, u32[]{:S(2)}) collective-permute-start(bf16[64,16,2048]{2,0,1:T(8,128)(2,1)} %broadcast_select_fusion.2), channel_id=1, source_target_pairs={{1,0},{2,1},{3,2},{4,3},{5,4},{6,5},{7,6},{9,8},{10,9},{11,10},{12... | collective-permute-start | bytes 12582920 | tf_op jit(solution)/shard_map/ppermute | solution.py:10
  207.9 99.3 %copy-start = (f32[8]{0:T(128)S(1)}, f32[8]{0:T(128)}, u32[]{:S(2)}) copy-start(f32[8]{0:T(128)} %param.14) | copy-start | bytes 100
  207.9 99.3 %copy-start.1 = (f32[8]{0:T(128)S(1)}, f32[8]{0:T(128)}, u32[]{:S(2)}) copy-start(f32[8]{0:T(128)} %param.12) | copy-start | bytes 100
  207.9 99.3 %copy-start.2 = (f32[8]{0:T(128)S(1)}, f32[8]{0:T(128)}, u32[]{:S(2)}) copy-start(f32[8]{0:T(128)} %param.13) | copy-start | bytes 100
where the time goes:
time: 858 us; the launch traced here: 852 us
  other arithmetic  442 us (52%)
  waiting for transfers between devices  279 us (33%)
  local copies, waits for them, and re-layouts  112 us (13%)
  loops' own time  11.7 us (1%)
    ppermute x3, waiting for transfers between devices, from_behind(): return lax.ppermute(block, axis, route)  279 us
    mul x8, other arithmetic, advance(): weight = jnp.exp(-(depth_sum[None] + before)) * (1.0 - jnp.exp(-optical))  139 us
    mul x8, other arithmetic, classify(): return (optical * inv_depth, emission)  135 us
    exp x8, other arithmetic, classify(): jnp.exp(-jnp.square(samples - centers[lobe_index]) * widths[lobe_index])  90.8 us
    exp x64, local copies, waits for them, and re-layouts, classify(): jnp.exp(-jnp.square(samples - centers[lobe_index]) * widths[lobe_index])  39.2 us
    another operation x8, other arithmetic, advance(): inclusive = jnp.cumsum(optical, axis=0)  37.4 us
  transfers between devices with their start and end apart: 3, of which 3 were waited for; matrix products, arithmetic and copies ran while one was open for 0% of the time, Pallas kernels for 0%

commit v1 on v0

v1 whole, which is shorter than its diff:
```python
import functools
import jax, jax.numpy as jnp
from jax import lax
from jax.experimental import pallas as pl
from jax.experimental.pallas import tpu as pltpu
from jax.sharding import PartitionSpec as P

LANES = 128
SUB = 8
LOG2E = 1.4426950408889634
LN2 = 0.6931471805599453
CHANNELS = 4


def compose_kernel(first, last, chunk_start, slices, rows, halo, inv_depth, unroll,
                   meta, shifts, sign_own, centers, widths, extinct, colors,
                   own, recv, below, above, *rest):
    if first:
        state_in, (out, scratch) = None, rest
    else:
        state_in, out, scratch = rest
    lobes = centers.shape[0]
    band = 2 * rows
    filled = halo + band + halo
    tail = scratch.shape[1] - filled
    parity, tile_lo, tile_hi = meta[0], meta[1], meta[2]
    shift_base = meta[3] + chunk_start
    at_own = pl.multiple_of(halo + parity * rows, SUB)
    at_recv = pl.multiple_of(halo + rows - parity * rows, SUB)

    def splat(v):
        return jnp.full((SUB, LANES), v, jnp.float32)

    gain = [splat(extinct[k]) * (LOG2E * inv_depth) for k in range(lobes)]
    slope = [jnp.sqrt(splat(widths[k]) * LOG2E) for k in range(lobes)]
    offset = [slope[k] * splat(centers[k]) for k in range(lobes)]
    level = [jnp.log(gain[k]) * LOG2E for k in range(lobes)]

    @pl.when(pl.program_id(0) == 0)
    def _():
        scratch[:, filled:, :] = jnp.zeros((scratch.shape[0], tail, LANES), jnp.float32)

    for cb in range(recv.shape[-1] // LANES):
        cols = slice(cb * LANES, (cb + 1) * LANES)

        def fill(s, carry):
            scratch[s, 0:halo, :] = below[s, :, cols].astype(jnp.float32)
            scratch[s, pl.ds(at_own, rows), :] = own[s, :, cols].astype(jnp.float32)
            scratch[s, pl.ds(at_recv, rows), :] = recv[s, :, cols].astype(jnp.float32)
            scratch[s, halo + band:filled, :] = above[s, :, cols].astype(jnp.float32)
            return carry

        lax.fori_loop(0, slices, fill, 0, unroll=2)
        if first:
            scratch[slices, 0:halo, :] = below[slices, :, cols].astype(jnp.float32)
            scratch[slices, pl.ds(at_own, rows), :] = jnp.full((rows, LANES), sign_own[0], jnp.float32)
            scratch[slices, pl.ds(at_recv, rows), :] = recv[slices, :, cols].astype(jnp.float32)

        def tile(t, carry):
            row = pl.multiple_of(t * SUB, SUB)
            here = pl.ds(row, SUB)
            if first:
                sign = scratch[slices, here, :]
                depth = jnp.zeros((SUB, LANES), jnp.float32)
                acc = [jnp.zeros((SUB, LANES), jnp.float32) for _ in range(lobes)]
            else:
                sign = state_in[lobes + 1, here, cols]
                depth = state_in[lobes, here, cols]
                acc = [state_in[k, here, cols] for k in range(lobes)]
            trans = jnp.exp2(depth * sign)

            def body(j, c):
                depth, trans, acc = c
                for u in range(unroll):
                    s = j * unroll + u
                    x = scratch[s, pl.ds(shifts[shift_base + s] + row, SUB), :]
                    lobe = []
                    optical = None
                    for k in range(lobes):
                        t_k = x * slope[k] - offset[k]
                        e = jnp.exp2(level[k] - t_k * t_k)
                        lobe.append(e)
                        optical = e if optical is None else optical + e
                    depth = depth + optical
                    new = jnp.exp2(depth * sign)
                    step = new - trans
                    acc = [acc[k] + step * lobe[k] for k in range(lobes)]
                    trans = new
                return depth, trans, acc

            depth, trans, acc = lax.fori_loop(0, slices // unroll, body, (depth, trans, acc))
            if last:
                norm = jnp.where(sign < 0, splat(-1.0), 1.0 / trans)
                for c in range(colors.shape[0]):
                    total = None
                    for k in range(lobes):
                        term = acc[k] * (splat(colors[c, k]) / gain[k])
                        total = term if total is None else total + term
                    out[c, here, cols] = total * norm
                out[CHANNELS - 1, here, cols] = depth * LN2
                out[CHANNELS, here, cols] = sign
            else:
                for k in range(lobes):
                    out[k, here, cols] = acc[k]
                out[lobes, here, cols] = depth
                out[lobes + 1, here, cols] = sign
            return carry

        lax.fori_loop(tile_lo, tile_hi, tile, 0)


def compose(meta, shifts, sign_own, params, volume, recv, below, above, state,
            *, first, last, part, chunk_start, slices, width, inv_depth, unroll):
    rows = volume.shape[1]
    halo = below.shape[1]
    band = 2 * rows
    cols = recv.shape[2]
    out_rows = band + halo
    lobes = params[0].shape[0]
    steps = cols // width
    half = steps // 2
    extra = 1 if first else 0
    cidx = chunk_start // slices
    smem = pl.BlockSpec(memory_space=pltpu.SMEM)

    def local_col(g, meta):
        if part is None:
            return g
        return (meta[4] if part else 1 - meta[4]) * half + g

    def own_map(g, meta, shifts):
        g = local_col(g, meta)
        return (cidx, 0, (g // half) * (2 * half) + meta[0] * half + g % half)

    def plain(g, meta, shifts):
        return (0, 0, local_col(g, meta))

    in_specs = [smem] * 5 + [
        pl.BlockSpec((slices, rows, width), own_map),
        pl.BlockSpec((slices + extra, rows, width), plain),
        pl.BlockSpec((slices + extra, halo, width), plain),
        pl.BlockSpec((slices, halo, width), plain),
    ]
    args = [sign_own, *params, volume, recv, below, above]
    aliases = {}
    if not first:
        in_specs.append(pl.BlockSpec((lobes + 2, out_rows, width), plain))
        args.append(state)
    if not first and not last:
        aliases = {2 + len(args) - 1: 0}
    n_out = CHANNELS + 1 if last else lobes + 2
    out_cols = cols if part is None else cols // 2
    samples = slices * out_rows * out_cols
    return pl.pallas_call(
        functools.partial(compose_kernel, first, last, chunk_start, slices, rows, halo, inv_depth, unroll),
        out_shape=jax.ShapeDtypeStruct((n_out, out_rows, out_cols), jnp.float32),
        grid_spec=pltpu.PrefetchScalarGridSpec(
            num_scalar_prefetch=2,
            grid=(steps if part is None else half,),
            in_specs=in_specs,
            out_specs=pl.BlockSpec((n_out, out_rows, width), lambda g, meta, shifts: (0, 0, g)),
            scratch_shapes=[pltpu.VMEM((slices + extra, halo + band + halo + halo, LANES), jnp.float32)],
        ),
        input_output_aliases=aliases,
        cost_estimate=pl.CostEstimate(flops=samples * 60, transcendentals=samples * 9, bytes_accessed=samples * 3),
        name="compose_first" if first else "compose_last" if last else "compose_mid",
    )(meta, shifts, *args)


def merge_kernel(rows, lead, meta, mine, got, here, side, up, cross, image):
    parity, slab = meta[0], meta[4]
    image[:, 0:lead, :] = jnp.zeros((CHANNELS, lead, image.shape[2]), jnp.float32)
    a_sum, b_sum = mine[CHANNELS - 1], got[CHANNELS - 1]
    first = jnp.where(slab == 0, -1.0, 1.0) * mine[CHANNELS] > 0
    through = jnp.exp(-jnp.where(first, a_sum, b_sum))
    for c in range(CHANNELS - 1):
        a, b = mine[c], got[c]
        image[c, lead:, :] = jnp.where(first, a, b) + through * jnp.where(first, b, a)
    image[CHANNELS - 1, lead:, :] = 1.0 - jnp.exp(-(a_sum + b_sum))
    band = 2 * rows

    def rows_at(start):
        return image[:, pl.ds(pl.multiple_of(start, SUB), rows), :]

    here[...] = rows_at(band + rows * parity)
    side[...] = rows_at(band + rows - rows * parity)
    up[...] = rows_at(rows * parity)
    cross[...] = rows_at(rows - rows * parity)


def merge(meta, mine, got, rows, lead):
    out_rows, cols = mine.shape[1:]
    width = 2 * LANES
    spec = pl.BlockSpec((CHANNELS, rows, width), lambda g, meta: (0, 0, g))
    shape = jax.ShapeDtypeStruct((CHANNELS, rows, cols), jnp.float32)
    return pl.pallas_call(
        functools.partial(merge_kernel, rows, lead),
        out_shape=[shape] * 4,
        grid_spec=pltpu.PrefetchScalarGridSpec(
            num_scalar_prefetch=1,
            grid=(cols // width,),
            in_specs=[
                pl.BlockSpec((CHANNELS + 1, out_rows, width), lambda g, meta: (0, 0, g)),
                pl.BlockSpec((CHANNELS, out_rows, width), lambda g, meta: (0, 0, g)),
            ],
            out_specs=[spec] * 4,
            scratch_shapes=[pltpu.VMEM((CHANNELS, lead + out_rows, width), jnp.float32)],
        ),
        name="merge",
    )(meta, mine, got)


CHUNKS = 4


def local(volume, shift_table, slab_order, centers, widths, extinct, colors):
    slab_count = lax.axis_size("depth")
    slab = lax.axis_index("depth")
    n = lax.axis_size("lat")
    me = lax.axis_index("lat")
    pair, parity = me // 2, me % 2
    slice_count, rows, col_count = volume.shape
    band = 2 * rows
    halo = 3 * rows // 2
    quarter = col_count // 4
    inv_depth = 1.0 / (slice_count * slab_count)
    chunk = slice_count // CHUNKS
    swap = [(i, i ^ 1) for i in range(n)]
    down = [(i, i - 2) for i in range(2, n)]
    up = [(i - 2, i) for i in range(2, n)]
    cross = [(i, (i ^ 1) - 2) for i in range(2, n)]
    is_last = pair == n // 2 - 1
    meta = jnp.stack([
        parity,
        jnp.where(pair == 0, halo // SUB, 0),
        jnp.where(is_last, (band + halo) // SUB, band // SUB),
        slab * slice_count,
        slab,
    ]).astype(jnp.int32)
    sign_own = jnp.where(slab_order[:, 0] == 0, -1.0, 1.0)
    params = (centers, widths, extinct, colors)

    def half(block, which):
        parts = [
            lax.dynamic_slice_in_dim(block, s * 2 * quarter + which * quarter, quarter, 2)
            for s in range(2)
        ]
        return jnp.concatenate(parts, axis=2)

    state = None
    for c in range(CHUNKS):
        block = volume[c * chunk:(c + 1) * chunk]
        give, own = half(block, 1 - parity), half(block, parity)
        if c == 0:
            flag = jnp.full((1, rows, 2 * quarter), sign_own[0], volume.dtype)
            give, own = jnp.concatenate([give, flag]), jnp.concatenate([own, flag])
        recv = lax.ppermute(give, "lat", swap)
        even = jnp.where(parity == 0, own, recv)
        odd = jnp.where(parity == 0, recv, own)
        upper = jnp.concatenate([even, odd[:, :halo - rows]], axis=1)[:chunk]
        lower = jnp.concatenate([even[:, band - halo:], odd], axis=1)
        above = lax.ppermute(upper, "lat", down)
        below = lax.ppermute(lower, "lat", up)
        run = functools.partial(
            compose, meta, shift_table, sign_own, params, volume, recv, below, above, state,
            first=c == 0, last=c == CHUNKS - 1, chunk_start=c * chunk, slices=chunk, width=2 * LANES,
            inv_depth=inv_depth, unroll=16)
        if c < CHUNKS - 1:
            state = run(part=None)
        else:
            give = run(part=0)
            mine = run(part=1)
    got = lax.ppermute(give[:CHANNELS], "depth", [(0, 1), (1, 0)])
    lead = band - halo
    from_pair, side, upper, diagonal = merge(meta, mine, got, rows, lead)
    from_side = lax.ppermute(side, "lat", swap)
    from_up = lax.ppermute(upper, "lat", down)
    from_cross = lax.ppermute(diagonal, "lat", cross)
    index = rows * parity + jnp.arange(rows)
    inside = (is_last | (index < lead))[None, :, None]
    a = jnp.where(inside, from_pair, from_up)
    b = jnp.where(inside, from_side, from_cross)
    return jnp.where(parity == 0, jnp.concatenate([a, b], axis=2), jnp.concatenate([b, a], axis=2))


def solution(mesh):
    in_specs = (
        P(("views", "depth"), "lat", None),
        P("views"),
        P(("views", "lat"), None),
        P(),
        P(),
        P(),
        P(),
    )
    out_specs = P(None, ("views", "lat"), "depth")

    return jax.shard_map(local, mesh=mesh, in_specs=in_specs, out_specs=out_specs, check_vma=False)
```

time: 858 us -> 153 us (0.18)
  the two profiles are of different devices: /device:TPU:0 before, /device:TPU:19 now
where the time goes in v1:
time: 153 us; the launch traced here: 152 us
  waiting for transfers between devices  48.6 us (32%)
  Pallas kernels  41.4 us (27%)
  starting transfers between devices  37.8 us (25%)
  local copies, waits for them, and re-layouts  12.8 us (8%)
  other arithmetic  10.7 us (7%)
    pallas_call x5, Pallas kernels, compose(): pl.pallas_call(functools.partial(compose_kernel, first, last, chunk_start...  38.7 us
    ppermute x4, waiting for transfers between devices, local(): recv = lax.ppermute(give, 'lat', swap)  25.7 us
    ppermute x1, waiting for transfers between devices, local(): from_up = lax.ppermute(upper, 'lat', down)  14.5 us
    ppermute x4, starting transfers between devices, local(): below = lax.ppermute(lower, 'lat', up)  13.8 us
    ppermute x4, starting transfers between devices, local(): above = lax.ppermute(upper, 'lat', down)  8.29 us
    ppermute x1, starting transfers between devices, local(): got = lax.ppermute(give[:CHANNELS], 'depth', [(0, 1), (1, 0)])  7.47 us
    ppermute x4, waiting for transfers between devices, local(): above = lax.ppermute(upper, 'lat', down)  4.59 us
    unnamed x26, local copies, waits for them, and re-layouts  4.35 us
  transfers between devices with their start and end apart: 16, of which 7 were waited for; matrix products, arithmetic and copies ran while one was open for 6% of the time, Pallas kernels for 22%

profile of v1, /device:TPU:19, one launch (start us, length us, event | category | flops | bytes accessed | tf_op | source)
XLA Modules:
  0.0 151.8 jit_solution(10091130830301899019)
XLA Ops:
  0.0 3.6 %fusion.6 = (bf16[16,16,2048]{2,1,0:T(8,128)(2,1)S(1)}, bf16[16,16,2048]{2,1,0:T(8,128)(2,1)}, bf16[16,16,2048]{2,1,0:T(8,128)(2,1)S(1)}, bf16[16,16,2048]{2,1,0:T(8,128)(2,1)S(1)}) fusion(bf16[64,16,2048]{2,1,0:T(8,128)(2,1)} %own.9), kind=kLoop, calls=%fused_computation.49 | loop fusion | bytes 8388608 | tf_op jit(solution)/shard_map/slice | solution.py:252
  3.6 2.2 %constant_dynamic-slice_fusion.1 = (bf16[16,16,512]{2,1,0:T(8,128)(2,1)}, bf16[16,16,512]{2,1,0:T(8,128)(2,1)}, bf16[16,16,512]{2,1,0:T(8,128)(2,1)S(1)}, bf16[1...) fusion(bf16[16,16,2048]{2,1,0:T(8,128)(2,1)S(1)} %get-tuple-ele, ...), kind=kLoop, calls=%fused_computation.33 | loop fusion | bytes 4194320 | tf_op jit(solution)/shard_map/dynamic_slice | solution.py:245
  12.4 7.3 %collective-permute-done.6.recv = bf16[16,16,1024]{2,1,0:T(8,128)(2,1)} collective-permute-done((bf16[16,16,1024]{2,1,0:T(8,128)(2,1)}, bf16[16,16,1024]{2,1,0:T(8,128)(2,1)}, u32[]{:S(2)}, u32[]{:S(2)}) %collective-permute-start.6) | collective-permute-done | bytes 524320 | tf_op jit(solution)/shard_map/ppermute | solution.py:257
  21.2 2.1 %collective-permute-start.8 = (bf16[16,24,1024]{2,1,0:T(8,128)(2,1)S(1)}, bf16[16,24,1024]{2,1,0:T(8,128)(2,1)S(1)}, u32[]{:S(2)}, u32[]{:S(2)}) collective-permute-start(bf16[16,24,1024]{2,1,0:T(8,128)(2,1)S(1)} %pad_maximum_fusion.7), channel_id=1, source_target_pairs={{2,0},{3,1},{4,2},{5,3},{6,4},{7,5},{10,8},{11,9},{12,10},{13,11},... | collective-permute-start | bytes 2359304 | tf_op jit(solution)/shard_map/ppermute | solution.py:262
  24.2 3.2 %collective-permute-start.7 = (bf16[16,24,1024]{2,1,0:T(8,128)(2,1)}, bf16[16,24,1024]{2,1,0:T(8,128)(2,1)}, u32[]{:S(2)}, u32[]{:S(2)}) collective-permute-start(bf16[16,24,1024]{2,1,0:T(8,128)(2,1)} %pad_maximum_fusion.6), channel_id=1, source_target_pairs={{0,2},{1,3},{2,4},{3,5},{4,6},{5,7},{8,10},{9,11},{10,12},{11,13},... | collective-permute-start | bytes 2359304 | tf_op jit(solution)/shard_map/ppermute | solution.py:263
  27.5 15.4 %collective-permute-done.3.recv = bf16[16,16,1024]{2,1,0:T(8,128)(2,1)S(1)} collective-permute-done((bf16[16,16,1024]{2,1,0:T(8,128)(2,1)S(1)}, bf16[16,16,1024]{2,1,0:T(8,128)(2,1)S(1)}, u32[]{:S(2)}, u32[]{:S(2)}) %collective-permute-start.3) | collective-permute-done | bytes 524320 | tf_op jit(solution)/shard_map/ppermute | solution.py:257
  45.6 3.2 %collective-permute-start.10 = (bf16[17,24,1024]{2,1,0:T(8,128)(2,1)S(1)}, bf16[17,24,1024]{2,1,0:T(8,128)(2,1)S(1)}, u32[]{:S(2)}, u32[]{:S(2)}) collective-permute-start(bf16[17,24,1024]{2,1,0:T(8,128)(2,1)S(1)} %pad_maximum_fusion), channel_id=1, source_target_pairs={{0,2},{1,3},{2,4},{3,5},{4,6},{5,7},{8,10},{9,11},{10,12},{11,13},... | collective-permute-start | bytes 2506760 | tf_op jit(solution)/shard_map/ppermute | solution.py:263
  48.9 2.1 %collective-permute-start.11 = (bf16[16,24,1024]{2,1,0:T(8,128)(2,1)S(1)}, bf16[16,24,1024]{2,1,0:T(8,128)(2,1)S(1)}, u32[]{:S(2)}, u32[]{:S(2)}) collective-permute-start(bf16[16,24,1024]{2,1,0:T(8,128)(2,1)S(1)} %pad_maximum_fusion.1), channel_id=1, source_target_pairs={{2,0},{3,1},{4,2},{5,3},{6,4},{7,5},{10,8},{11,9},{12,10},{13,11},... | collective-permute-start | bytes 2359304 | tf_op jit(solution)/shard_map/ppermute | solution.py:262
  51.0 3.0 %collective-permute-done.recv = bf16[16,16,1024]{2,1,0:T(8,128)(2,1)S(1)} collective-permute-done((bf16[16,16,1024]{2,1,0:T(8,128)(2,1)}, bf16[16,16,1024]{2,1,0:T(8,128)(2,1)S(1)}, u32[]{:S(2)}, u32[]{:S(2)}) %collective-permute-start) | collective-permute-done | bytes 524320 | tf_op jit(solution)/shard_map/ppermute | solution.py:257
  54.0 2.1 %collective-permute-start.5 = (bf16[16,24,1024]{2,1,0:T(8,128)(2,1)S(1)}, bf16[16,24,1024]{2,1,0:T(8,128)(2,1)}, u32[]{:S(2)}, u32[]{:S(2)}) collective-permute-start(bf16[16,24,1024]{2,1,0:T(8,128)(2,1)S(1)} %pad_maximum_fusion.5), channel_id=1, source_target_pairs={{2,0},{3,1},{4,2},{5,3},{6,4},{7,5},{10,8},{11,9},{12,10},{13,11},... | collective-permute-start | bytes 2359304 | tf_op jit(solution)/shard_map/ppermute | solution.py:262
  57.5 4.1 %collective-permute-start.4 = (bf16[16,24,1024]{2,1,0:T(8,128)(2,1)}, bf16[16,24,1024]{2,1,0:T(8,128)(2,1)}, u32[]{:S(2)}, u32[]{:S(2)}) collective-permute-start(bf16[16,24,1024]{2,1,0:T(8,128)(2,1)} %pad_maximum_fusion.4), channel_id=1, source_target_pairs={{0,2},{1,3},{2,4},{3,5},{4,6},{5,7},{8,10},{9,11},{10,12},{11,13},... | collective-permute-start | bytes 2359304 | tf_op jit(solution)/shard_map/ppermute | solution.py:263
  62.6 4.4 %collective-permute-done.11.above = bf16[16,24,1024]{2,1,0:T(8,128)(2,1)S(1)} collective-permute-done((bf16[16,24,1024]{2,1,0:T(8,128)(2,1)S(1)}, bf16[16,24,1024]{2,1,0:T(8,128)(2,1)S(1)}, u32[]{:S(2)}, u32[]{:S(2)}) %collective-permute-start.11) | collective-permute-done | bytes 786464 | tf_op jit(solution)/shard_map/ppermute | solution.py:262
  67.0 2.1 %collective-permute-start.2 = (bf16[16,24,1024]{2,1,0:T(8,128)(2,1)S(1)}, bf16[16,24,1024]{2,1,0:T(8,128)(2,1)S(1)}, u32[]{:S(2)}, u32[]{:S(2)}) collective-permute-start(bf16[16,24,1024]{2,1,0:T(8,128)(2,1)S(1)} %pad_maximum_fusion.3), channel_id=1, source_target_pairs={{2,0},{3,1},{4,2},{5,3},{6,4},{7,5},{10,8},{11,9},{12,10},{13,11},... | collective-permute-start | bytes 2359304 | tf_op jit(solution)/shard_map/ppermute | solution.py:262
  70.0 3.2 %collective-permute-start.1 = (bf16[16,24,1024]{2,1,0:T(8,128)(2,1)}, bf16[16,24,1024]{2,1,0:T(8,128)(2,1)S(1)}, u32[]{:S(2)}, u32[]{:S(2)}) collective-permute-start(bf16[16,24,1024]{2,1,0:T(8,128)(2,1)} %pad_maximum_fusion.2), channel_id=1, source_target_pairs={{0,2},{1,3},{2,4},{3,5},{4,6},{5,7},{8,10},{9,11},{10,12},{11,13},... | collective-permute-start | bytes 2359304 | tf_op jit(solution)/shard_map/ppermute | solution.py:263
  73.9 8.7 %compose_first.1.rest_0_ = f32[10,56,1024]{2,1,0:T(8,128)} custom-call(s32[5]{0:T(128)} %stack.23.meta, s32[128]{0:T(128)} %shifts.9, f32[1]{0:T(128)} %bitcast.5.sign_own, f32[8]{0:T(128)} %centers.9, f32[8]{0:T(128)} %widths.9, f32[8]{0:T(128)} %extinct.9, f32[3,8]{1,0:T(4,128)} %colors.9, bf16[64,16,2048]{2,1,0:T(8,128)(2,1)} %own.9, ...), custom_call_target="tpu_custom_call" | custom-call | flops 55050240 | bytes 2752512 | tf_op jit(solution)/shard_map/compose_first/pallas_call | solution.py:154
  82.6 9.0 %compose_mid.2.rest_0_ = f32[10,56,1024]{2,1,0:T(8,128)} custom-call(s32[5]{0:T(128)} %stack.23.meta, s32[128]{0:T(128)} %shifts.9, f32[1]{0:T(128)} %bitcast.5.sign_own, f32[8]{0:T(128)} %centers.9, f32[8]{0:T(128)} %widths.9, f32[8]{0:T(128)} %extinct.9, f32[3,8]{1,0:T(4,128)} %colors.9, ...), custom_call_target="tpu_custom_call", output_to_operand_aliasing={{}: (11, {})} | custom-call | flops 55050240 | bytes 2752512 | tf_op jit(solution)/shard_map/compose_mid/pallas_call | solution.py:154
  91.6 9.0 %compose_mid.3.rest_0_ = f32[10,56,1024]{2,1,0:T(8,128)} custom-call(s32[5]{0:T(128)} %stack.23.meta, s32[128]{0:T(128)} %shifts.9, f32[1]{0:T(128)} %bitcast.5.sign_own, f32[8]{0:T(128)} %centers.9, f32[8]{0:T(128)} %widths.9, f32[8]{0:T(128)} %extinct.9, f32[3,8]{1,0:T(4,128)} %colors.9, ...), custom_call_target="tpu_custom_call", output_to_operand_aliasing={{}: (11, {})} | custom-call | flops 55050240 | bytes 2752512 | tf_op jit(solution)/shard_map/compose_mid/pallas_call | solution.py:154
  102.5 6.0 %compose_last.3 = f32[5,56,512]{2,1,0:T(8,128)} custom-call(s32[5]{0:T(128)} %stack.23.meta, s32[128]{0:T(128)} %shifts.9, f32[1]{0:T(128)} %bitcast.5.sign_own, f32[8]{0:T(128)} %centers.9, f32[8]{0:T(128)} %widths.9, f32[8]{0:T(128)} %extinct.9, f32[3,8]{1,0:T(4,128)} %colors.9, bf16[64,16,2048]{2,1,0:T(8,128)(2,1)} %own.9, bf16[16,16,1024]{2,1,0:T(8,128)(2,1)} %copy-done, ...), custom_call_target="tpu_custom_call" | custom-call | flops 27525120 | bytes 1376256 | tf_op jit(solution)/shard_map/compose_last/pallas_call | solution.py:154
  109.6 7.5 %collective-permute-start.12 = (f32[4,56,512]{2,1,0:T(8,128)S(1)}, f32[4,56,512]{2,1,0:T(8,128)S(1)}, u32[]{:S(2)}, u32[]{:S(2)}) collective-permute-start(f32[4,56,512]{2,1,0:T(8,128)S(1)} %slice.68), channel_id=1, source_target_pairs={{0,8},{8,0},{1,9},{9,1},{2,10},{10,2},{3,11},{11,3},{4,12},{12,4},... | collective-permute-start | bytes 1376264 | tf_op jit(solution)/shard_map/ppermute | solution.py:273
  117.1 6.0 %compose_last.2.mine = f32[5,56,512]{2,1,0:T(8,128)} custom-call(s32[5]{0:T(128)} %stack.23.meta, s32[128]{0:T(128)} %shifts.9, f32[1]{0:T(128)} %bitcast.5.sign_own, f32[8]{0:T(128)} %centers.9, f32[8]{0:T(128)} %widths.9, f32[8]{0:T(128)} %extinct.9, f32[3,8]{1,0:T(4,128)} %colors.9, bf16[64,16,2048]{2,1,0:T(8,128)(2,1)} %own.9, ...), custom_call_target="tpu_custom_call" | custom-call | flops 27525120 | bytes 1376256 | tf_op jit(solution)/shard_map/compose_last/pallas_call | solution.py:154
  123.9 2.7 %merge.1 = (f32[4,16,512]{2,1,0:T(8,128)}, f32[4,16,512]{2,1,0:T(8,128)}, f32[4,16,512]{2,1,0:T(8,128)}, f32[4,16,512]{2,1,0:T(8,128)}) custom-call(s32[5]{0:T(128)} %stack.23.meta, f32[5,56,512]{2,1,0:T(8,128)} %compose_last.2.mine, f32[4,56,512]{2,1,0:T(8,128)} %copy-done.8), custom_call_target="tpu_custom_call" | custom-call | tf_op jit(solution)/shard_map/merge/pallas_call | solution.py:196
  126.5 2.0 %collective-permute-start.13 = (f32[4,16,512]{2,1,0:T(8,128)}, f32[4,16,512]{2,1,0:T(8,128)S(1)}, u32[]{:S(2)}, u32[]{:S(2)}) collective-permute-start(f32[4,16,512]{2,1,0:T(8,128)} %get-tuple-element.10), channel_id=1, source_target_pairs={{2,0},{3,1},{4,2},{5,3},{6,4},{7,5},{10,8},{11,9},{12,10},{13,11},... | collective-permute-start | bytes 393224 | tf_op jit(solution)/shard_map/ppermute | solution.py:277
  131.8 14.5 %collective-permute-done.13 = f32[4,16,512]{2,1,0:T(8,128)S(1)} collective-permute-done((f32[4,16,512]{2,1,0:T(8,128)}, f32[4,16,512]{2,1,0:T(8,128)S(1)}, u32[]{:S(2)}, u32[]{:S(2)}) %collective-permute-start.13) | collective-permute-done | bytes 131104 | tf_op jit(solution)/shard_map/ppermute | solution.py:277
  146.3 3.8 %collective-permute-done.15 = f32[4,16,512]{2,1,0:T(8,128)S(1)} collective-permute-done((f32[4,16,512]{2,1,0:T(8,128)}, f32[4,16,512]{2,1,0:T(8,128)S(1)}, u32[]{:S(2)}, u32[]{:S(2)}) %collective-permute-start.15) | collective-permute-done | bytes 131104 | tf_op jit(solution)/shard_map/ppermute | solution.py:278
  (72 shorter events, 24.2 us)
Async XLA Ops:
  3.6 4.3 %copy-start.12 = (s32[1,2]{1,0:T(1,128)S(1)}, s32[1,2]{1,0:T(1,128)}, u32[]{:S(2)}) copy-start(s32[1,2]{1,0:T(1,128)} %param.9) | copy-start | bytes 28
  6.6 13.1 %collective-permute-start.6 = (bf16[16,16,1024]{2,1,0:T(8,128)(2,1)}, bf16[16,16,1024]{2,1,0:T(8,128)(2,1)}, u32[]{:S(2)}, u32[]{:S(2)}) collective-permute-start(bf16[16,16,1024]{2,1,0:T(8,128)(2,1)} %pad_maximum_fusion.12), channel_id=1, source_target_pairs={{0,1},{1,0},{2,3},{3,2},{4,5},{5,4},{6,7},{7,6},{8,9},{9,8},{10,11... | collective-permute-start | bytes 1572872 | tf_op jit(solution)/shard_map/ppermute | solution.py:257
  8.8 34.9 %collective-permute-start.9 = (bf16[17,16,1024]{2,1,0:T(8,128)(2,1)}, bf16[17,16,1024]{2,1,0:T(8,128)(2,1)}, u32[]{:S(2)}, u32[]{:S(2)}) collective-permute-start(bf16[17,16,1024]{2,1,0:T(8,128)(2,1)} %fusion.4), channel_id=1, source_target_pairs={{0,1},{1,0},{2,3},{3,2},{4,5},{5,4},{6,7},{7,6},{8,9},{9,8},{10,11... | collective-permute-start | bytes 1671176 | tf_op jit(solution)/shard_map/ppermute | solution.py:257
  10.0 9.8 %copy-start.3 = (bf16[16,16,512]{2,1,0:T(8,128)(2,1)S(1)}, bf16[16,16,512]{2,1,0:T(8,128)(2,1)}, u32[]{:S(2)}) copy-start(bf16[16,16,512]{2,1,0:T(8,128)(2,1)} %get-tuple-element.46) | copy-start | bytes 786436
  10.0 32.9 %collective-permute-start.3 = (bf16[16,16,1024]{2,1,0:T(8,128)(2,1)S(1)}, bf16[16,16,1024]{2,1,0:T(8,128)(2,1)S(1)}, u32[]{:S(2)}, u32[]{:S(2)}) collective-permute-start(bf16[16,16,1024]{2,1,0:T(8,128)(2,1)S(1)} %pad_maximum_fusion.10), channel_id=1, source_target_pairs={{0,1},{1,0},{2,3},{3,2},{4,5},{5,4},{6,7},{7,6},{8,9},{9,8},{10,11... | collective-permute-start | bytes 1572872 | tf_op jit(solution)/shard_map/ppermute | solution.py:257
  12.2 41.8 %collective-permute-start = (bf16[16,16,1024]{2,1,0:T(8,128)(2,1)}, bf16[16,16,1024]{2,1,0:T(8,128)(2,1)S(1)}, u32[]{:S(2)}, u32[]{:S(2)}) collective-permute-start(bf16[16,16,1024]{2,1,0:T(8,128)(2,1)} %pad_maximum_fusion.8), channel_id=1, source_target_pairs={{0,1},{1,0},{2,3},{3,2},{4,5},{5,4},{6,7},{7,6},{8,9},{9,8},{10,11... | collective-permute-start | bytes 1572872 | tf_op jit(solution)/shard_map/ppermute | solution.py:257
  21.1 21.8 %copy-start.4 = (bf16[16,16,512]{2,1,0:T(8,128)(2,1)S(1)}, bf16[16,16,512]{2,1,0:T(8,128)(2,1)}, u32[]{:S(2)}) copy-start(bf16[16,16,512]{2,1,0:T(8,128)(2,1)} %get-tuple-element.32) | copy-start | bytes 786436
  21.2 36.3 %collective-permute-start.8 = (bf16[16,24,1024]{2,1,0:T(8,128)(2,1)S(1)}, bf16[16,24,1024]{2,1,0:T(8,128)(2,1)S(1)}, u32[]{:S(2)}, u32[]{:S(2)}) collective-permute-start(bf16[16,24,1024]{2,1,0:T(8,128)(2,1)S(1)} %pad_maximum_fusion.7), channel_id=1, source_target_pairs={{2,0},{3,1},{4,2},{5,3},{6,4},{7,5},{10,8},{11,9},{12,10},{13,11},... | collective-permute-start | bytes 2359304 | tf_op jit(solution)/shard_map/ppermute | solution.py:262
  24.2 58.4 %collective-permute-start.7 = (bf16[16,24,1024]{2,1,0:T(8,128)(2,1)}, bf16[16,24,1024]{2,1,0:T(8,128)(2,1)}, u32[]{:S(2)}, u32[]{:S(2)}) collective-permute-start(bf16[16,24,1024]{2,1,0:T(8,128)(2,1)} %pad_maximum_fusion.6), channel_id=1, source_target_pairs={{0,2},{1,3},{2,4},{3,5},{4,6},{5,7},{8,10},{9,11},{10,12},{11,13},... | collective-permute-start | bytes 2359304 | tf_op jit(solution)/shard_map/ppermute | solution.py:263
  42.9 1.1 copy-start.5
  42.9 1.2 copy-start.6
  45.6 23.5 %collective-permute-start.10 = (bf16[17,24,1024]{2,1,0:T(8,128)(2,1)S(1)}, bf16[17,24,1024]{2,1,0:T(8,128)(2,1)S(1)}, u32[]{:S(2)}, u32[]{:S(2)}) collective-permute-start(bf16[17,24,1024]{2,1,0:T(8,128)(2,1)S(1)} %pad_maximum_fusion), channel_id=1, source_target_pairs={{0,2},{1,3},{2,4},{3,5},{4,6},{5,7},{8,10},{9,11},{10,12},{11,13},... | collective-permute-start | bytes 2506760 | tf_op jit(solution)/shard_map/ppermute | solution.py:263
  48.9 18.2 %collective-permute-start.11 = (bf16[16,24,1024]{2,1,0:T(8,128)(2,1)S(1)}, bf16[16,24,1024]{2,1,0:T(8,128)(2,1)S(1)}, u32[]{:S(2)}, u32[]{:S(2)}) collective-permute-start(bf16[16,24,1024]{2,1,0:T(8,128)(2,1)S(1)} %pad_maximum_fusion.1), channel_id=1, source_target_pairs={{2,0},{3,1},{4,2},{5,3},{6,4},{7,5},{10,8},{11,9},{12,10},{13,11},... | collective-permute-start | bytes 2359304 | tf_op jit(solution)/shard_map/ppermute | solution.py:262
  54.0 2.4 %copy-start = (bf16[16,16,1024]{2,1,0:T(8,128)(2,1)}, bf16[16,16,1024]{2,1,0:T(8,128)(2,1)S(1)}, u32[]{:S(2)}) copy-start(bf16[16,16,1024]{2,1,0:T(8,128)(2,1)S(1)} %collective-permute-done.recv) | copy-start | bytes 1572868
  54.0 37.5 %collective-permute-start.5 = (bf16[16,24,1024]{2,1,0:T(8,128)(2,1)S(1)}, bf16[16,24,1024]{2,1,0:T(8,128)(2,1)}, u32[]{:S(2)}, u32[]{:S(2)}) collective-permute-start(bf16[16,24,1024]{2,1,0:T(8,128)(2,1)S(1)} %pad_maximum_fusion.5), channel_id=1, source_target_pairs={{2,0},{3,1},{4,2},{5,3},{6,4},{7,5},{10,8},{11,9},{12,10},{13,11},... | collective-permute-start | bytes 2359304 | tf_op jit(solution)/shard_map/ppermute | solution.py:262
  57.5 11.6 %copy-start.10 = (bf16[16,24,1024]{2,1,0:T(8,128)(2,1)}, bf16[16,24,1024]{2,1,0:T(8,128)(2,1)S(1)}, u32[]{:S(2)}) copy-start(bf16[16,24,1024]{2,1,0:T(8,128)(2,1)S(1)} %collective-permute-done.8.above) | copy-start | bytes 2359300
  57.5 34.1 %collective-permute-start.4 = (bf16[16,24,1024]{2,1,0:T(8,128)(2,1)}, bf16[16,24,1024]{2,1,0:T(8,128)(2,1)}, u32[]{:S(2)}, u32[]{:S(2)}) collective-permute-start(bf16[16,24,1024]{2,1,0:T(8,128)(2,1)} %pad_maximum_fusion.4), channel_id=1, source_target_pairs={{0,2},{1,3},{2,4},{3,5},{4,6},{5,7},{8,10},{9,11},{10,12},{11,13},... | collective-permute-start | bytes 2359304 | tf_op jit(solution)/shard_map/ppermute | solution.py:263
  67.0 2.1 %copy-start.11 = (bf16[16,24,1024]{2,1,0:T(8,128)(2,1)}, bf16[16,24,1024]{2,1,0:T(8,128)(2,1)S(1)}, u32[]{:S(2)}) copy-start(bf16[16,24,1024]{2,1,0:T(8,128)(2,1)S(1)} %collective-permute-done.11.above) | copy-start | bytes 2359300
  67.0 33.7 %collective-permute-start.2 = (bf16[16,24,1024]{2,1,0:T(8,128)(2,1)S(1)}, bf16[16,24,1024]{2,1,0:T(8,128)(2,1)S(1)}, u32[]{:S(2)}, u32[]{:S(2)}) collective-permute-start(bf16[16,24,1024]{2,1,0:T(8,128)(2,1)S(1)} %pad_maximum_fusion.3), channel_id=1, source_target_pairs={{2,0},{3,1},{4,2},{5,3},{6,4},{7,5},{10,8},{11,9},{12,10},{13,11},... | collective-permute-start | bytes 2359304 | tf_op jit(solution)/shard_map/ppermute | solution.py:262
  70.0 30.7 %collective-permute-start.1 = (bf16[16,24,1024]{2,1,0:T(8,128)(2,1)}, bf16[16,24,1024]{2,1,0:T(8,128)(2,1)S(1)}, u32[]{:S(2)}, u32[]{:S(2)}) collective-permute-start(bf16[16,24,1024]{2,1,0:T(8,128)(2,1)} %pad_maximum_fusion.2), channel_id=1, source_target_pairs={{0,2},{1,3},{2,4},{3,5},{4,6},{5,7},{8,10},{9,11},{10,12},{11,13},... | collective-permute-start | bytes 2359304 | tf_op jit(solution)/shard_map/ppermute | solution.py:263
  109.6 13.5 %collective-permute-start.12 = (f32[4,56,512]{2,1,0:T(8,128)S(1)}, f32[4,56,512]{2,1,0:T(8,128)S(1)}, u32[]{:S(2)}, u32[]{:S(2)}) collective-permute-start(f32[4,56,512]{2,1,0:T(8,128)S(1)} %slice.68), channel_id=1, source_target_pairs={{0,8},{8,0},{1,9},{9,1},{2,10},{10,2},{3,11},{11,3},{4,12},{12,4},... | collective-permute-start | bytes 1376264 | tf_op jit(solution)/shard_map/ppermute | solution.py:273
  126.5 19.7 %collective-permute-start.13 = (f32[4,16,512]{2,1,0:T(8,128)}, f32[4,16,512]{2,1,0:T(8,128)S(1)}, u32[]{:S(2)}, u32[]{:S(2)}) collective-permute-start(f32[4,16,512]{2,1,0:T(8,128)} %get-tuple-element.10), channel_id=1, source_target_pairs={{2,0},{3,1},{4,2},{5,3},{6,4},{7,5},{10,8},{11,9},{12,10},{13,11},... | collective-permute-start | bytes 393224 | tf_op jit(solution)/shard_map/ppermute | solution.py:277
  128.6 17.7 %collective-permute-start.14 = (f32[4,16,512]{2,1,0:T(8,128)}, f32[4,16,512]{2,1,0:T(8,128)S(1)}, u32[]{:S(2)}, u32[]{:S(2)}) collective-permute-start(f32[4,16,512]{2,1,0:T(8,128)} %get-tuple-element.11), channel_id=1, source_target_pairs={{0,1},{1,0},{2,3},{3,2},{4,5},{5,4},{6,7},{7,6},{8,9},{9,8},{10,11... | collective-permute-start | bytes 393224 | tf_op jit(solution)/shard_map/ppermute | solution.py:276
  129.9 20.2 %collective-permute-start.15 = (f32[4,16,512]{2,1,0:T(8,128)}, f32[4,16,512]{2,1,0:T(8,128)S(1)}, u32[]{:S(2)}, u32[]{:S(2)}) collective-permute-start(f32[4,16,512]{2,1,0:T(8,128)} %get-tuple-element.12), channel_id=1, source_target_pairs={{2,1},{3,0},{4,3},{5,2},{6,5},{7,4},{10,9},{11,8},{12,11},{13,10},... | collective-permute-start | bytes 393224 | tf_op jit(solution)/shard_map/ppermute | solution.py:278
  (5 other events, 4.2 us)

commit v2 on v1

v2 whole, which is shorter than its diff:
```python
import functools
import jax, jax.numpy as jnp
from jax import lax
from jax.experimental import pallas as pl
from jax.experimental.pallas import tpu as pltpu
from jax.sharding import PartitionSpec as P

LANES = 128
SUB = 8
LOG2E = 1.4426950408889634
LN2 = 0.6931471805599453
CHANNELS = 4
PARITY, TILE_LO, TILE_HI, SHIFT_BASE, SLAB = range(5)
SMEM = pl.BlockSpec(memory_space=pltpu.SMEM)
VMEM = pl.BlockSpec(memory_space=pltpu.VMEM)
PARAMS = pltpu.CompilerParams(vmem_limit_bytes=24 * 2**20)


def lanes_at(start):
    return pl.ds(pl.multiple_of(start, LANES), LANES)


def volume_lane(block, blocks, which):
    per = blocks // 2
    slab = block // per
    return ((2 * slab + which) * per + block - slab * per) * LANES


def compose_kernel(first, last, part, chunk_start, slices, rows, halo, inv_depth, unroll,
                   meta, shifts, sign_own, centers, widths, extinct, colors,
                   volume, recv, below, above, *rest):
    if first:
        state_in, (out, scratch) = None, rest
    else:
        state_in, out, scratch = rest
    lobes = centers.shape[0]
    band = 2 * rows
    filled = halo + band + halo
    tail = scratch.shape[1] - filled
    parity, tile_lo, tile_hi = meta[PARITY], meta[TILE_LO], meta[TILE_HI]
    shift_base = meta[SHIFT_BASE] + chunk_start
    at_own = pl.multiple_of(halo + parity * rows, SUB)
    at_recv = pl.multiple_of(halo + rows - parity * rows, SUB)
    blocks = recv.shape[-1] // LANES

    def splat(v):
        return jnp.full((SUB, LANES), v, jnp.float32)

    gain = [splat(extinct[k]) * (LOG2E * inv_depth) for k in range(lobes)]
    slope = [jnp.sqrt(splat(widths[k]) * LOG2E) for k in range(lobes)]
    offset = [slope[k] * splat(centers[k]) for k in range(lobes)]
    level = [jnp.log(gain[k]) * LOG2E for k in range(lobes)]

    scratch[:, filled:, :] = jnp.zeros((scratch.shape[0], tail, LANES), jnp.float32)

    def column(block, carry):
        if part is None:
            source, target = block, block
        else:
            keep = meta[SLAB] if part else 1 - meta[SLAB]
            source, target = keep * (blocks // 2) + block, block
        cols = lanes_at(source * LANES)
        here_cols = lanes_at(target * LANES)
        own_cols = lanes_at(volume_lane(source, blocks, parity))

        def fill(s, carry):
            scratch[s, 0:halo, :] = below[s, :, cols].astype(jnp.float32)
            scratch[s, pl.ds(at_own, rows), :] = volume[chunk_start + s, :, own_cols].astype(jnp.float32)
            scratch[s, pl.ds(at_recv, rows), :] = recv[s, :, cols].astype(jnp.float32)
            scratch[s, halo + band:filled, :] = above[s, :, cols].astype(jnp.float32)
            return carry

        lax.fori_loop(0, slices, fill, 0, unroll=4)
        if first:
            scratch[slices, 0:halo, :] = below[slices, :, cols].astype(jnp.float32)
            scratch[slices, pl.ds(at_own, rows), :] = jnp.full((rows, LANES), sign_own[0], jnp.float32)
            scratch[slices, pl.ds(at_recv, rows), :] = recv[slices, :, cols].astype(jnp.float32)

        def tile(t, carry):
            row = pl.multiple_of(t * SUB, SUB)
            here = pl.ds(row, SUB)
            if first:
                sign = scratch[slices, here, :]
                depth = jnp.zeros((SUB, LANES), jnp.float32)
                acc = [jnp.zeros((SUB, LANES), jnp.float32) for _ in range(lobes)]
            else:
                sign = state_in[lobes + 1, here, cols]
                depth = state_in[lobes, here, cols]
                acc = [state_in[k, here, cols] for k in range(lobes)]
            trans = jnp.exp2(depth * sign)

            def body(j, c):
                depth, trans, acc = c
                for u in range(unroll):
                    s = j * unroll + u
                    x = scratch[s, pl.ds(shifts[shift_base + s] + row, SUB), :]
                    lobe = []
                    optical = None
                    for k in range(lobes):
                        t_k = x * slope[k] - offset[k]
                        e = jnp.exp2(level[k] - t_k * t_k)
                        lobe.append(e)
                        optical = e if optical is None else optical + e
                    depth = depth + optical
                    new = jnp.exp2(depth * sign)
                    step = new - trans
                    acc = [acc[k] + step * lobe[k] for k in range(lobes)]
                    trans = new
                return depth, trans, acc

            depth, trans, acc = lax.fori_loop(0, slices // unroll, body, (depth, trans, acc))
            if last:
                norm = jnp.where(sign < 0, splat(-1.0), 1.0 / trans)
                for c in range(colors.shape[0]):
                    total = None
                    for k in range(lobes):
                        term = acc[k] * (splat(colors[c, k]) / gain[k])
                        total = term if total is None else total + term
                    out[c, here, here_cols] = total * norm
                out[CHANNELS - 1, here, here_cols] = depth * LN2
                out[CHANNELS, here, here_cols] = sign
            else:
                for k in range(lobes):
                    out[k, here, here_cols] = acc[k]
                out[lobes, here, here_cols] = depth
                out[lobes + 1, here, here_cols] = sign
            return carry

        lax.fori_loop(tile_lo, tile_hi, tile, 0)
        return carry

    lax.fori_loop(0, blocks if part is None else blocks // 2, column, 0)


def compose(meta, shifts, sign_own, params, volume, recv, below, above, state,
            *, first, last, part, chunk_start, slices, inv_depth, unroll):
    rows = volume.shape[1]
    halo = below.shape[1]
    band = 2 * rows
    cols = recv.shape[2]
    out_rows = band + halo
    lobes = params[0].shape[0]
    args = [meta, shifts, sign_own, *params, volume, recv, below, above]
    specs = [SMEM] * 7 + [VMEM] * 4
    aliases = {}
    if not first:
        args.append(state)
        specs.append(VMEM)
        if not last:
            aliases = {len(args) - 1: 0}
    n_out = CHANNELS + 1 if last else lobes + 2
    out_cols = cols if part is None else cols // 2
    samples = slices * out_rows * out_cols
    return pl.pallas_call(
        functools.partial(compose_kernel, first, last, part, chunk_start, slices, rows, halo, inv_depth, unroll),
        out_shape=jax.ShapeDtypeStruct((n_out, out_rows, out_cols), jnp.float32),
        in_specs=specs,
        out_specs=VMEM,
        scratch_shapes=[pltpu.VMEM((slices + (1 if first else 0), filled_rows(rows, halo), LANES), jnp.float32)],
        input_output_aliases=aliases,
        compiler_params=PARAMS,
        cost_estimate=pl.CostEstimate(flops=samples * 60, transcendentals=samples * 9, bytes_accessed=samples * 3),
        name="compose_first" if first else "compose_last" if last else "compose_mid",
    )(*args)


def filled_rows(rows, halo):
    return 2 * rows + 3 * halo


def split_kernel(slices, chunk_start, meta, sign_own, volume, out):
    blocks = out.shape[2] // LANES
    other = 1 - meta[PARITY]
    for b in range(blocks):
        source = lanes_at(volume_lane(b, blocks, other))
        out[0:slices, :, b * LANES:(b + 1) * LANES] = volume[chunk_start:chunk_start + slices, :, source]
    if out.shape[0] > slices:
        sign = jnp.full((out.shape[1], out.shape[2]), sign_own[0], jnp.float32)
        out[slices] = sign.astype(out.dtype)


def split(meta, sign_own, volume, chunk_start, slices, first):
    rows, cols = volume.shape[1], volume.shape[2]
    total = slices + (1 if first else 0)
    return pl.pallas_call(
        functools.partial(split_kernel, slices, chunk_start),
        out_shape=jax.ShapeDtypeStruct((total, rows, cols // 2), volume.dtype),
        in_specs=[SMEM, SMEM, VMEM],
        out_specs=VMEM,
        compiler_params=PARAMS,
        cost_estimate=pl.CostEstimate(flops=0, transcendentals=0, bytes_accessed=2 * total * rows * cols),
        name="split",
    )(meta, sign_own, volume)


def pack_kernel(slices, chunk_start, rows, halo, meta, sign_own, volume, recv, upper, lower):
    blocks = recv.shape[2] // LANES
    odd_in_upper = halo - rows
    even_from = 2 * rows - halo
    flags = recv.shape[0] > slices
    parity = meta[PARITY]

    def place(own_is_even):
        for b in range(blocks):
            cols = slice(b * LANES, (b + 1) * LANES)
            source = lanes_at(volume_lane(b, blocks, parity))

            def one(s, carry):
                own = volume[chunk_start + s, :, source]
                other = recv[s, :, cols]
                even, odd = (own, other) if own_is_even else (other, own)
                upper[s, 0:rows, cols] = even
                upper[s, rows:halo, cols] = odd[0:odd_in_upper]
                lower[s, 0:halo - rows, cols] = even[even_from:rows]
                lower[s, halo - rows:halo, cols] = odd
                return carry

            lax.fori_loop(0, slices, one, 0, unroll=4)
        if flags:
            own = jnp.full((rows, lower.shape[2]), sign_own[0], jnp.float32).astype(lower.dtype)
            other = recv[slices]
            even, odd = (own, other) if own_is_even else (other, own)
            lower[slices, 0:halo - rows, :] = even[even_from:rows]
            lower[slices, halo - rows:halo, :] = odd

    @pl.when(parity == 0)
    def _():
        place(True)

    @pl.when(parity == 1)
    def _():
        place(False)


def pack(meta, sign_own, volume, recv, chunk_start, slices, halo):
    rows = volume.shape[1]
    total, _, cols = recv.shape
    return pl.pallas_call(
        functools.partial(pack_kernel, slices, chunk_start, rows, halo),
        out_shape=[
            jax.ShapeDtypeStruct((slices, halo, cols), recv.dtype),
            jax.ShapeDtypeStruct((total, halo, cols), recv.dtype),
        ],
        in_specs=[SMEM, SMEM, VMEM, VMEM],
        out_specs=[VMEM, VMEM],
        compiler_params=PARAMS,
        cost_estimate=pl.CostEstimate(flops=0, transcendentals=0, bytes_accessed=4 * total * rows * cols),
        name="pack",
    )(meta, sign_own, volume, recv)


def merge_kernel(rows, lead, meta, mine, got, here, side, up, cross, image):
    parity, slab = meta[PARITY], meta[SLAB]
    band = 2 * rows
    blocks = mine.shape[2] // LANES
    image[:, 0:lead, :] = jnp.zeros((CHANNELS, lead, LANES), jnp.float32)
    for b in range(blocks):
        cols = slice(b * LANES, (b + 1) * LANES)
        a_sum, b_sum = mine[CHANNELS - 1, :, cols], got[CHANNELS - 1, :, cols]
        first = jnp.where(slab == 0, -1.0, 1.0) * mine[CHANNELS, :, cols] > 0
        through = jnp.exp(-jnp.where(first, a_sum, b_sum))
        for c in range(CHANNELS - 1):
            a, g = mine[c, :, cols], got[c, :, cols]
            image[c, lead:, :] = jnp.where(first, a, g) + through * jnp.where(first, g, a)
        image[CHANNELS - 1, lead:, :] = 1.0 - jnp.exp(-(a_sum + b_sum))

        def rows_at(start):
            return image[:, pl.ds(pl.multiple_of(start, SUB), rows), :]

        here[:, :, cols] = rows_at(band + rows * parity)
        side[:, :, cols] = rows_at(band + rows - rows * parity)
        up[:, :, cols] = rows_at(rows * parity)
        cross[:, :, cols] = rows_at(rows - rows * parity)


def merge(meta, mine, got, rows, lead):
    out_rows, cols = mine.shape[1:]
    shape = jax.ShapeDtypeStruct((CHANNELS, rows, cols), jnp.float32)
    return pl.pallas_call(
        functools.partial(merge_kernel, rows, lead),
        out_shape=[shape] * 4,
        in_specs=[SMEM, VMEM, VMEM],
        out_specs=[VMEM] * 4,
        scratch_shapes=[pltpu.VMEM((CHANNELS, lead + out_rows, LANES), jnp.float32)],
        compiler_params=PARAMS,
        name="merge",
    )(meta, mine, got)


CHUNKS = (1, 2, 2, 2, 1)


def unroll_of(chunk):
    return max(u for u in range(1, 17) if chunk % u == 0)


def local(volume, shift_table, slab_order, centers, widths, extinct, colors):
    slab_count = lax.axis_size("depth")
    slab = lax.axis_index("depth")
    n = lax.axis_size("lat")
    me = lax.axis_index("lat")
    pair, parity = me // 2, me % 2
    slice_count, rows, _ = volume.shape
    band = 2 * rows
    halo = 3 * rows // 2
    inv_depth = 1.0 / (slice_count * slab_count)
    swap = [(i, i ^ 1) for i in range(n)]
    down = [(i, i - 2) for i in range(2, n)]
    up = [(i - 2, i) for i in range(2, n)]
    cross = [(i, (i ^ 1) - 2) for i in range(2, n)]
    is_last = pair == n // 2 - 1
    meta = jnp.stack([
        parity,
        jnp.where(pair == 0, halo // SUB, 0),
        jnp.where(is_last, (band + halo) // SUB, band // SUB),
        slab * slice_count,
        slab,
    ]).astype(jnp.int32)
    sign_own = jnp.where(slab_order[:, 0] == 0, -1.0, 1.0)
    params = (centers, widths, extinct, colors)

    state = None
    start = 0
    for c, part in enumerate(CHUNKS):
        chunk = slice_count * part // sum(CHUNKS)
        first, last = c == 0, c == len(CHUNKS) - 1
        give = split(meta, sign_own, volume, start, chunk, first)
        recv = lax.ppermute(give, "lat", swap)
        upper, lower = pack(meta, sign_own, volume, recv, start, chunk, halo)
        above = lax.ppermute(upper, "lat", down)
        below = lax.ppermute(lower, "lat", up)
        run = functools.partial(
            compose, meta, shift_table, sign_own, params, volume, recv, below, above, state,
            first=first, last=last, chunk_start=start, slices=chunk,
            inv_depth=inv_depth, unroll=unroll_of(chunk))
        if last:
            give = run(part=0)
            mine = run(part=1)
        else:
            state = run(part=None)
        start += chunk
    got = lax.ppermute(give, "depth", [(0, 1), (1, 0)])
    lead = band - halo
    from_pair, side, upper, diagonal = merge(meta, mine, got, rows, lead)
    from_side = lax.ppermute(side, "lat", swap)
    from_up = lax.ppermute(upper, "lat", down)
    from_cross = lax.ppermute(diagonal, "lat", cross)
    index = rows * parity + jnp.arange(rows)
    inside = (is_last | (index < lead))[None, :, None]
    a = jnp.where(inside, from_pair, from_up)
    b = jnp.where(inside, from_side, from_cross)
    return jnp.where(parity == 0, jnp.concatenate([a, b], axis=2), jnp.concatenate([b, a], axis=2))


def solution(mesh):
    in_specs = (
        P(("views", "depth"), "lat", None),
        P("views"),
        P(("views", "lat"), None),
        P(),
        P(),
        P(),
        P(),
    )
    out_specs = P(None, ("views", "lat"), "depth")

    return jax.shard_map(local, mesh=mesh, in_specs=in_specs, out_specs=out_specs, check_vma=False)
```

time: 153 us -> 144 us (0.941)
  the two profiles are of different devices: /device:TPU:19 before, /device:TPU:0 now
where the time goes in v2:
time: 144 us; the launch traced here: 142 us
  waiting for transfers between devices  77 us (53%)
  starting transfers between devices  39.4 us (27%)
  Pallas kernels  21.5 us (15%)
  local copies, waits for them, and re-layouts  2.31 us (2%)
    ppermute x5, waiting for transfers between devices, local(): above = lax.ppermute(upper, 'lat', down)  36.5 us
    ppermute x5, waiting for transfers between devices, local(): recv = lax.ppermute(give, 'lat', swap)  29.6 us
    ppermute x5, starting transfers between devices, local(): below = lax.ppermute(lower, 'lat', up)  21.3 us
    pallas_call x6, Pallas kernels, compose(): pl.pallas_call(functools.partial(compose_kernel, first, last, part, chunk...  12.8 us
    ppermute x5, starting transfers between devices, local(): recv = lax.ppermute(give, 'lat', swap)  7.39 us
    ppermute x1, waiting for transfers between devices, local(): from_up = lax.ppermute(upper, 'lat', down)  6.54 us
    ppermute x5, starting transfers between devices, local(): above = lax.ppermute(upper, 'lat', down)  6.45 us
    pallas_call x5, Pallas kernels, pack(): pl.pallas_call(functools.partial(pack_kernel, slices, chunk_start, rows,...  4.57 us
  transfers between devices with their start and end apart: 19, of which 10 were waited for; matrix products, arithmetic and copies ran while one was open for 0% of the time, Pallas kernels for 13%

profile of v2, /device:TPU:0, one launch (start us, length us, event | category | flops | bytes accessed | tf_op | source)
XLA Modules:
  0.0 142.0 jit_solution(6541944928393548102)
XLA Ops:
  0.7 2.2 %copy-done = bf16[64,16,2048]{2,1,0:T(8,128)(2,1)S(1)} copy-done((bf16[64,16,2048]{2,1,0:T(8,128)(2,1)S(1)}, bf16[64,16,2048]{2,1,0:T(8,128)(2,1)}, u32[]{:S(2)}) %copy-start) | copy-done | bytes 4194328
  3.6 3.1 %collective-permute-start.9 = (bf16[16,16,1024]{2,1,0:T(8,128)(2,1)S(1)}, bf16[16,16,1024]{2,1,0:T(8,128)(2,1)S(1)}, u32[]{:S(2)}, u32[]{:S(2)}) collective-permute-start(bf16[16,16,1024]{2,1,0:T(8,128)(2,1)S(1)} %split.8), channel_id=1, source_target_pairs={{0,1},{1,0},{2,3},{3,2},{4,5},{5,4},{6,7},{7,6},{8,9},{9,8},{10,11... | collective-permute-start | bytes 1572872 | tf_op jit(solution)/shard_map/ppermute | solution.py:328
  8.2 2.1 %collective-permute-start.3 = (bf16[16,16,1024]{2,1,0:T(8,128)(2,1)S(1)}, bf16[16,16,1024]{2,1,0:T(8,128)(2,1)S(1)}, u32[]{:S(2)}, u32[]{:S(2)}) collective-permute-start(bf16[16,16,1024]{2,1,0:T(8,128)(2,1)S(1)} %split.6), channel_id=1, source_target_pairs={{0,1},{1,0},{2,3},{3,2},{4,5},{5,4},{6,7},{7,6},{8,9},{9,8},{10,11... | collective-permute-start | bytes 1572872 | tf_op jit(solution)/shard_map/ppermute | solution.py:328
  10.3 9.2 %collective-permute-done.9.recv = bf16[16,16,1024]{2,1,0:T(8,128)(2,1)S(1)} collective-permute-done((bf16[16,16,1024]{2,1,0:T(8,128)(2,1)S(1)}, bf16[16,16,1024]{2,1,0:T(8,128)(2,1)S(1)}, u32[]{:S(2)}, u32[]{:S(2)}) %collective-permute-start.9) | collective-permute-done | bytes 524320 | tf_op jit(solution)/shard_map/ppermute | solution.py:328
  20.5 4.0 %collective-permute-start.10 = (bf16[16,24,1024]{2,1,0:T(8,128)(2,1)S(1)}, bf16[16,24,1024]{2,1,0:T(8,128)(2,1)S(1)}, u32[]{:S(2)}, u32[]{:S(2)}) collective-permute-start(bf16[16,24,1024]{2,1,0:T(8,128)(2,1)S(1)} %get-tuple-element.25), channel_id=1, source_target_pairs={{0,2},{1,3},{2,4},{3,5},{4,6},{5,7},{8,10},{9,11},{10,12},{11,13},... | collective-permute-start | bytes 2359304 | tf_op jit(solution)/shard_map/ppermute | solution.py:331
  25.1 1.6 %collective-permute-start.12 = (bf16[9,16,1024]{2,1,0:T(8,128)(2,1)S(1)}, bf16[9,16,1024]{2,1,0:T(8,128)(2,1)S(1)}, u32[]{:S(2)}, u32[]{:S(2)}) collective-permute-start(bf16[9,16,1024]{2,1,0:T(8,128)(2,1)S(1)} %split.9), channel_id=1, source_target_pairs={{0,1},{1,0},{2,3},{3,2},{4,5},{5,4},{6,7},{7,6},{8,9},{9,8},{10,11... | collective-permute-start | bytes 884744 | tf_op jit(solution)/shard_map/ppermute | solution.py:328
  27.9 20.3 %collective-permute-done.12.recv = bf16[9,16,1024]{2,1,0:T(8,128)(2,1)S(1)} collective-permute-done((bf16[9,16,1024]{2,1,0:T(8,128)(2,1)S(1)}, bf16[9,16,1024]{2,1,0:T(8,128)(2,1)S(1)}, u32[]{:S(2)}, u32[]{:S(2)}) %collective-permute-start.12) | collective-permute-done | bytes 294944 | tf_op jit(solution)/shard_map/ppermute | solution.py:328
  49.1 4.0 %collective-permute-start.13 = (bf16[9,24,1024]{2,1,0:T(8,128)(2,1)S(1)}, bf16[9,24,1024]{2,1,0:T(8,128)(2,1)S(1)}, u32[]{:S(2)}, u32[]{:S(2)}) collective-permute-start(bf16[9,24,1024]{2,1,0:T(8,128)(2,1)S(1)} %get-tuple-element.27), channel_id=1, source_target_pairs={{0,2},{1,3},{2,4},{3,5},{4,6},{5,7},{8,10},{9,11},{10,12},{11,13},... | collective-permute-start | bytes 1327112 | tf_op jit(solution)/shard_map/ppermute | solution.py:331
  56.7 5.2 %collective-permute-start.7 = (bf16[16,24,1024]{2,1,0:T(8,128)(2,1)S(1)}, bf16[16,24,1024]{2,1,0:T(8,128)(2,1)S(1)}, u32[]{:S(2)}, u32[]{:S(2)}) collective-permute-start(bf16[16,24,1024]{2,1,0:T(8,128)(2,1)S(1)} %get-tuple-element.23), channel_id=1, source_target_pairs={{0,2},{1,3},{2,4},{3,5},{4,6},{5,7},{8,10},{9,11},{10,12},{11,13},... | collective-permute-start | bytes 2359304 | tf_op jit(solution)/shard_map/ppermute | solution.py:331
  61.9 5.0 %collective-permute-done.14.above = bf16[8,24,1024]{2,1,0:T(8,128)(2,1)S(1)} collective-permute-done((bf16[8,24,1024]{2,1,0:T(8,128)(2,1)S(1)}, bf16[8,24,1024]{2,1,0:T(8,128)(2,1)S(1)}, u32[]{:S(2)}, u32[]{:S(2)}) %collective-permute-start.14) | collective-permute-done | bytes 393248 | tf_op jit(solution)/shard_map/ppermute | solution.py:330
  69.3 4.6 %collective-permute-start.4 = (bf16[16,24,1024]{2,1,0:T(8,128)(2,1)S(1)}, bf16[16,24,1024]{2,1,0:T(8,128)(2,1)S(1)}, u32[]{:S(2)}, u32[]{:S(2)}) collective-permute-start(bf16[16,24,1024]{2,1,0:T(8,128)(2,1)S(1)} %get-tuple-element.21), channel_id=1, source_target_pairs={{0,2},{1,3},{2,4},{3,5},{4,6},{5,7},{8,10},{9,11},{10,12},{11,13},... | collective-permute-start | bytes 2359304 | tf_op jit(solution)/shard_map/ppermute | solution.py:331
  76.0 7.8 %collective-permute-done.11.above = bf16[16,24,1024]{2,1,0:T(8,128)(2,1)S(1)} collective-permute-done((bf16[16,24,1024]{2,1,0:T(8,128)(2,1)S(1)}, bf16[16,24,1024]{2,1,0:T(8,128)(2,1)S(1)}, u32[]{:S(2)}, u32[]{:S(2)}) %collective-permute-start.11) | collective-permute-done | bytes 786464 | tf_op jit(solution)/shard_map/ppermute | solution.py:330
  83.8 3.5 %collective-permute-start.1 = (bf16[8,24,1024]{2,1,0:T(8,128)(2,1)S(1)}, bf16[8,24,1024]{2,1,0:T(8,128)(2,1)S(1)}, u32[]{:S(2)}, u32[]{:S(2)}) collective-permute-start(bf16[8,24,1024]{2,1,0:T(8,128)(2,1)S(1)} %get-tuple-element.19), channel_id=1, source_target_pairs={{0,2},{1,3},{2,4},{3,5},{4,6},{5,7},{8,10},{9,11},{10,12},{11,13},... | collective-permute-start | bytes 1179656 | tf_op jit(solution)/shard_map/ppermute | solution.py:331
  88.7 1.8 %compose_first.1.rest_0_ = f32[10,56,1024]{2,1,0:T(8,128)S(1)} custom-call(s32[5]{0:T(128)S(1)} %stack.23.meta, s32[128]{0:T(128)S(1)} %copy-done.2, f32[1]{0:T(128)} %bitcast.5.sign_own, f32[8]{0:T(128)S(1)} %copy-done.3, f32[8]{0:T(128)S(1)} %copy-done.4, f32[8]{0:T(128)S(1)} %copy-done.5, f32[3,8]{1,0:T(4,128)S(1)} %copy-done.1, ...), custom_call_target="tpu_custom_call" | custom-call | flops 27525120 | bytes 1376256 | tf_op jit(solution)/shard_map/compose_first/pallas_call | solution.py:154
  90.5 2.8 %compose_mid.3.rest_0_ = f32[10,56,1024]{2,1,0:T(8,128)S(1)} custom-call(s32[5]{0:T(128)S(1)} %stack.23.meta, s32[128]{0:T(128)S(1)} %copy-done.2, f32[1]{0:T(128)} %bitcast.5.sign_own, f32[8]{0:T(128)S(1)} %copy-done.3, f32[8]{0:T(128)S(1)} %copy-done.4, f32[8]{0:T(128)S(1)} %copy-done.5, f32[3,8]{1,0:T(4,128)S(1)} %copy-done.1, ...), custom_call_target="tpu_custom_call", output_to_operand_aliasing={{}: (11, {})} | custom-call | flops 55050240 | bytes 2752512 | tf_op jit(solution)/shard_map/compose_mid/pallas_call | solution.py:154
  93.3 7.4 %collective-permute-done.8.above = bf16[16,24,1024]{2,1,0:T(8,128)(2,1)S(1)} collective-permute-done((bf16[16,24,1024]{2,1,0:T(8,128)(2,1)S(1)}, bf16[16,24,1024]{2,1,0:T(8,128)(2,1)S(1)}, u32[]{:S(2)}, u32[]{:S(2)}) %collective-permute-start.8) | collective-permute-done | bytes 786464 | tf_op jit(solution)/shard_map/ppermute | solution.py:330
  100.7 2.8 %compose_mid.4.rest_0_ = f32[10,56,1024]{2,1,0:T(8,128)S(1)} custom-call(s32[5]{0:T(128)S(1)} %stack.23.meta, s32[128]{0:T(128)S(1)} %copy-done.2, f32[1]{0:T(128)} %bitcast.5.sign_own, f32[8]{0:T(128)S(1)} %copy-done.3, f32[8]{0:T(128)S(1)} %copy-done.4, f32[8]{0:T(128)S(1)} %copy-done.5, f32[3,8]{1,0:T(4,128)S(1)} %copy-done.1, ...), custom_call_target="tpu_custom_call", output_to_operand_aliasing={{}: (11, {})} | custom-call | flops 55050240 | bytes 2752512 | tf_op jit(solution)/shard_map/compose_mid/pallas_call | solution.py:154
  103.5 14.0 %collective-permute-done.5.above = bf16[16,24,1024]{2,1,0:T(8,128)(2,1)S(1)} collective-permute-done((bf16[16,24,1024]{2,1,0:T(8,128)(2,1)S(1)}, bf16[16,24,1024]{2,1,0:T(8,128)(2,1)S(1)}, u32[]{:S(2)}, u32[]{:S(2)}) %collective-permute-start.5) | collective-permute-done | bytes 786464 | tf_op jit(solution)/shard_map/ppermute | solution.py:330
  117.5 2.8 %compose_mid.5.rest_0_ = f32[10,56,1024]{2,1,0:T(8,128)S(1)} custom-call(s32[5]{0:T(128)S(1)} %stack.23.meta, s32[128]{0:T(128)S(1)} %copy-done.2, f32[1]{0:T(128)} %bitcast.5.sign_own, f32[8]{0:T(128)S(1)} %copy-done.3, f32[8]{0:T(128)S(1)} %copy-done.4, f32[8]{0:T(128)S(1)} %copy-done.5, f32[3,8]{1,0:T(4,128)S(1)} %copy-done.1, ...), custom_call_target="tpu_custom_call", output_to_operand_aliasing={{}: (11, {})} | custom-call | flops 55050240 | bytes 2752512 | tf_op jit(solution)/shard_map/compose_mid/pallas_call | solution.py:154
  120.3 2.2 %collective-permute-done.2.above = bf16[8,24,1024]{2,1,0:T(8,128)(2,1)S(1)} collective-permute-done((bf16[8,24,1024]{2,1,0:T(8,128)(2,1)S(1)}, bf16[8,24,1024]{2,1,0:T(8,128)(2,1)S(1)}, u32[]{:S(2)}, u32[]{:S(2)}) %collective-permute-start.2) | collective-permute-done | bytes 393248 | tf_op jit(solution)/shard_map/ppermute | solution.py:330
  124.0 1.3 compose_last.2.mine
  128.0 1.6 %collective-permute-start.17 = (f32[4,16,512]{2,1,0:T(8,128)S(1)}, f32[4,16,512]{2,1,0:T(8,128)S(1)}, u32[]{:S(2)}, u32[]{:S(2)}) collective-permute-start(f32[4,16,512]{2,1,0:T(8,128)S(1)} %get-tuple-element.31), channel_id=1, source_target_pairs={{0,1},{1,0},{2,3},{3,2},{4,5},{5,4},{6,7},{7,6},{8,9},{9,8},{10,11... | collective-permute-start | bytes 393224 | tf_op jit(solution)/shard_map/ppermute | solution.py:345
  130.9 6.5 %collective-permute-done.16 = f32[4,16,512]{2,1,0:T(8,128)S(1)} collective-permute-done((f32[4,16,512]{2,1,0:T(8,128)S(1)}, f32[4,16,512]{2,1,0:T(8,128)S(1)}, u32[]{:S(2)}, u32[]{:S(2)}) %collective-permute-start.16) | collective-permute-done | bytes 131104 | tf_op jit(solution)/shard_map/ppermute | solution.py:346
  137.4 3.8 %collective-permute-done.18 = f32[4,16,512]{2,1,0:T(8,128)S(1)} collective-permute-done((f32[4,16,512]{2,1,0:T(8,128)S(1)}, f32[4,16,512]{2,1,0:T(8,128)S(1)}, u32[]{:S(2)}, u32[]{:S(2)}) %collective-permute-start.18) | collective-permute-done | bytes 131104 | tf_op jit(solution)/shard_map/ppermute | solution.py:347
  (47 shorter events, 21.3 us)
Async XLA Ops:
  3.6 15.8 %collective-permute-start.9 = (bf16[16,16,1024]{2,1,0:T(8,128)(2,1)S(1)}, bf16[16,16,1024]{2,1,0:T(8,128)(2,1)S(1)}, u32[]{:S(2)}, u32[]{:S(2)}) collective-permute-start(bf16[16,16,1024]{2,1,0:T(8,128)(2,1)S(1)} %split.8), channel_id=1, source_target_pairs={{0,1},{1,0},{2,3},{3,2},{4,5},{5,4},{6,7},{7,6},{8,9},{9,8},{10,11... | collective-permute-start | bytes 1572872 | tf_op jit(solution)/shard_map/ppermute | solution.py:328
  7.4 45.7 %collective-permute-start.6 = (bf16[16,16,1024]{2,1,0:T(8,128)(2,1)S(1)}, bf16[16,16,1024]{2,1,0:T(8,128)(2,1)S(1)}, u32[]{:S(2)}, u32[]{:S(2)}) collective-permute-start(bf16[16,16,1024]{2,1,0:T(8,128)(2,1)S(1)} %split.7), channel_id=1, source_target_pairs={{0,1},{1,0},{2,3},{3,2},{4,5},{5,4},{6,7},{7,6},{8,9},{9,8},{10,11... | collective-permute-start | bytes 1572872 | tf_op jit(solution)/shard_map/ppermute | solution.py:328
  8.2 48.5 %collective-permute-start.3 = (bf16[16,16,1024]{2,1,0:T(8,128)(2,1)S(1)}, bf16[16,16,1024]{2,1,0:T(8,128)(2,1)S(1)}, u32[]{:S(2)}, u32[]{:S(2)}) collective-permute-start(bf16[16,16,1024]{2,1,0:T(8,128)(2,1)S(1)} %split.6), channel_id=1, source_target_pairs={{0,1},{1,0},{2,3},{3,2},{4,5},{5,4},{6,7},{7,6},{8,9},{9,8},{10,11... | collective-permute-start | bytes 1572872 | tf_op jit(solution)/shard_map/ppermute | solution.py:328
  20.5 53.5 %collective-permute-start.10 = (bf16[16,24,1024]{2,1,0:T(8,128)(2,1)S(1)}, bf16[16,24,1024]{2,1,0:T(8,128)(2,1)S(1)}, u32[]{:S(2)}, u32[]{:S(2)}) collective-permute-start(bf16[16,24,1024]{2,1,0:T(8,128)(2,1)S(1)} %get-tuple-element.25), channel_id=1, source_target_pairs={{0,2},{1,3},{2,4},{3,5},{4,6},{5,7},{8,10},{9,11},{10,12},{11,13},... | collective-permute-start | bytes 2359304 | tf_op jit(solution)/shard_map/ppermute | solution.py:331
  25.1 23.1 %collective-permute-start.12 = (bf16[9,16,1024]{2,1,0:T(8,128)(2,1)S(1)}, bf16[9,16,1024]{2,1,0:T(8,128)(2,1)S(1)}, u32[]{:S(2)}, u32[]{:S(2)}) collective-permute-start(bf16[9,16,1024]{2,1,0:T(8,128)(2,1)S(1)} %split.9), channel_id=1, source_target_pairs={{0,1},{1,0},{2,3},{3,2},{4,5},{5,4},{6,7},{7,6},{8,9},{9,8},{10,11... | collective-permute-start | bytes 884744 | tf_op jit(solution)/shard_map/ppermute | solution.py:328
  27.4 28.0 %collective-permute-start = (bf16[8,16,1024]{2,1,0:T(8,128)(2,1)S(1)}, bf16[8,16,1024]{2,1,0:T(8,128)(2,1)S(1)}, u32[]{:S(2)}, u32[]{:S(2)}) collective-permute-start(bf16[8,16,1024]{2,1,0:T(8,128)(2,1)S(1)} %split.5), channel_id=1, source_target_pairs={{0,1},{1,0},{2,3},{3,2},{4,5},{5,4},{6,7},{7,6},{8,9},{9,8},{10,11... | collective-permute-start | bytes 786440 | tf_op jit(solution)/shard_map/ppermute | solution.py:328
  49.1 20.3 %collective-permute-start.13 = (bf16[9,24,1024]{2,1,0:T(8,128)(2,1)S(1)}, bf16[9,24,1024]{2,1,0:T(8,128)(2,1)S(1)}, u32[]{:S(2)}, u32[]{:S(2)}) collective-permute-start(bf16[9,24,1024]{2,1,0:T(8,128)(2,1)S(1)} %get-tuple-element.27), channel_id=1, source_target_pairs={{0,2},{1,3},{2,4},{3,5},{4,6},{5,7},{8,10},{9,11},{10,12},{11,13},... | collective-permute-start | bytes 1327112 | tf_op jit(solution)/shard_map/ppermute | solution.py:331
  53.1 13.9 %collective-permute-start.14 = (bf16[8,24,1024]{2,1,0:T(8,128)(2,1)S(1)}, bf16[8,24,1024]{2,1,0:T(8,128)(2,1)S(1)}, u32[]{:S(2)}, u32[]{:S(2)}) collective-permute-start(bf16[8,24,1024]{2,1,0:T(8,128)(2,1)S(1)} %get-tuple-element.28), channel_id=1, source_target_pairs={{2,0},{3,1},{4,2},{5,3},{6,4},{7,5},{10,8},{11,9},{12,10},{13,11},... | collective-permute-start | bytes 1179656 | tf_op jit(solution)/shard_map/ppermute | solution.py:330
  55.4 28.4 %collective-permute-start.11 = (bf16[16,24,1024]{2,1,0:T(8,128)(2,1)S(1)}, bf16[16,24,1024]{2,1,0:T(8,128)(2,1)S(1)}, u32[]{:S(2)}, u32[]{:S(2)}) collective-permute-start(bf16[16,24,1024]{2,1,0:T(8,128)(2,1)S(1)} %get-tuple-element.26), channel_id=1, source_target_pairs={{2,0},{3,1},{4,2},{5,3},{6,4},{7,5},{10,8},{11,9},{12,10},{13,11},... | collective-permute-start | bytes 2359304 | tf_op jit(solution)/shard_map/ppermute | solution.py:330
  56.7 30.6 %collective-permute-start.7 = (bf16[16,24,1024]{2,1,0:T(8,128)(2,1)S(1)}, bf16[16,24,1024]{2,1,0:T(8,128)(2,1)S(1)}, u32[]{:S(2)}, u32[]{:S(2)}) collective-permute-start(bf16[16,24,1024]{2,1,0:T(8,128)(2,1)S(1)} %get-tuple-element.23), channel_id=1, source_target_pairs={{0,2},{1,3},{2,4},{3,5},{4,6},{5,7},{8,10},{9,11},{10,12},{11,13},... | collective-permute-start | bytes 2359304 | tf_op jit(solution)/shard_map/ppermute | solution.py:331
  67.0 33.7 %collective-permute-start.8 = (bf16[16,24,1024]{2,1,0:T(8,128)(2,1)S(1)}, bf16[16,24,1024]{2,1,0:T(8,128)(2,1)S(1)}, u32[]{:S(2)}, u32[]{:S(2)}) collective-permute-start(bf16[16,24,1024]{2,1,0:T(8,128)(2,1)S(1)} %get-tuple-element.24), channel_id=1, source_target_pairs={{2,0},{3,1},{4,2},{5,3},{6,4},{7,5},{10,8},{11,9},{12,10},{13,11},... | collective-permute-start | bytes 2359304 | tf_op jit(solution)/shard_map/ppermute | solution.py:330
  69.3 19.3 %copy-start.1 = (f32[3,8]{1,0:T(4,128)S(1)}, f32[3,8]{1,0:T(4,128)}, u32[]{:S(2)}) copy-start(f32[3,8]{1,0:T(4,128)} %colors.11) | copy-start | bytes 292
  69.3 19.3 %copy-start.2 = (s32[128]{0:T(128)S(1)}, s32[128]{0:T(128)}, u32[]{:S(2)}) copy-start(s32[128]{0:T(128)} %shifts.11) | copy-start | bytes 1540
  69.3 19.3 %copy-start.3 = (f32[8]{0:T(128)S(1)}, f32[8]{0:T(128)}, u32[]{:S(2)}) copy-start(f32[8]{0:T(128)} %centers.11) | copy-start | bytes 100
  69.3 19.3 %copy-start.4 = (f32[8]{0:T(128)S(1)}, f32[8]{0:T(128)}, u32[]{:S(2)}) copy-start(f32[8]{0:T(128)} %widths.11) | copy-start | bytes 100
  69.3 19.3 %copy-start.5 = (f32[8]{0:T(128)S(1)}, f32[8]{0:T(128)}, u32[]{:S(2)}) copy-start(f32[8]{0:T(128)} %extinct.11) | copy-start | bytes 100
  69.3 34.1 %collective-permute-start.4 = (bf16[16,24,1024]{2,1,0:T(8,128)(2,1)S(1)}, bf16[16,24,1024]{2,1,0:T(8,128)(2,1)S(1)}, u32[]{:S(2)}, u32[]{:S(2)}) collective-permute-start(bf16[16,24,1024]{2,1,0:T(8,128)(2,1)S(1)} %get-tuple-element.21), channel_id=1, source_target_pairs={{0,2},{1,3},{2,4},{3,5},{4,6},{5,7},{8,10},{9,11},{10,12},{11,13},... | collective-permute-start | bytes 2359304 | tf_op jit(solution)/shard_map/ppermute | solution.py:331
  74.0 43.6 %collective-permute-start.5 = (bf16[16,24,1024]{2,1,0:T(8,128)(2,1)S(1)}, bf16[16,24,1024]{2,1,0:T(8,128)(2,1)S(1)}, u32[]{:S(2)}, u32[]{:S(2)}) collective-permute-start(bf16[16,24,1024]{2,1,0:T(8,128)(2,1)S(1)} %get-tuple-element.22), channel_id=1, source_target_pairs={{2,0},{3,1},{4,2},{5,3},{6,4},{7,5},{10,8},{11,9},{12,10},{13,11},... | collective-permute-start | bytes 2359304 | tf_op jit(solution)/shard_map/ppermute | solution.py:330
  83.8 36.5 %collective-permute-start.1 = (bf16[8,24,1024]{2,1,0:T(8,128)(2,1)S(1)}, bf16[8,24,1024]{2,1,0:T(8,128)(2,1)S(1)}, u32[]{:S(2)}, u32[]{:S(2)}) collective-permute-start(bf16[8,24,1024]{2,1,0:T(8,128)(2,1)S(1)} %get-tuple-element.19), channel_id=1, source_target_pairs={{0,2},{1,3},{2,4},{3,5},{4,6},{5,7},{8,10},{9,11},{10,12},{11,13},... | collective-permute-start | bytes 1179656 | tf_op jit(solution)/shard_map/ppermute | solution.py:331
  87.3 35.2 %collective-permute-start.2 = (bf16[8,24,1024]{2,1,0:T(8,128)(2,1)S(1)}, bf16[8,24,1024]{2,1,0:T(8,128)(2,1)S(1)}, u32[]{:S(2)}, u32[]{:S(2)}) collective-permute-start(bf16[8,24,1024]{2,1,0:T(8,128)(2,1)S(1)} %get-tuple-element.20), channel_id=1, source_target_pairs={{2,0},{3,1},{4,2},{5,3},{6,4},{7,5},{10,8},{11,9},{12,10},{13,11},... | collective-permute-start | bytes 1179656 | tf_op jit(solution)/shard_map/ppermute | solution.py:330
  123.9 2.0 %collective-permute-start.15 = (f32[5,56,512]{2,1,0:T(8,128)S(1)}, f32[5,56,512]{2,1,0:T(8,128)S(1)}, u32[]{:S(2)}, u32[]{:S(2)}) collective-permute-start(f32[5,56,512]{2,1,0:T(8,128)S(1)} %compose_last.3), channel_id=1, source_target_pairs={{0,8},{8,0},{1,9},{9,1},{2,10},{10,2},{3,11},{11,3},{4,12},{12,4},... | collective-permute-start | bytes 1720328 | tf_op jit(solution)/shard_map/ppermute | solution.py:342
  126.7 10.7 %collective-permute-start.16 = (f32[4,16,512]{2,1,0:T(8,128)S(1)}, f32[4,16,512]{2,1,0:T(8,128)S(1)}, u32[]{:S(2)}, u32[]{:S(2)}) collective-permute-start(f32[4,16,512]{2,1,0:T(8,128)S(1)} %get-tuple-element.30), channel_id=1, source_target_pairs={{2,0},{3,1},{4,2},{5,3},{6,4},{7,5},{10,8},{11,9},{12,10},{13,11},... | collective-permute-start | bytes 393224 | tf_op jit(solution)/shard_map/ppermute | solution.py:346
  128.0 9.4 %collective-permute-start.17 = (f32[4,16,512]{2,1,0:T(8,128)S(1)}, f32[4,16,512]{2,1,0:T(8,128)S(1)}, u32[]{:S(2)}, u32[]{:S(2)}) collective-permute-start(f32[4,16,512]{2,1,0:T(8,128)S(1)} %get-tuple-element.31), channel_id=1, source_target_pairs={{0,1},{1,0},{2,3},{3,2},{4,5},{5,4},{6,7},{7,6},{8,9},{9,8},{10,11... | collective-permute-start | bytes 393224 | tf_op jit(solution)/shard_map/ppermute | solution.py:345
  129.6 11.6 %collective-permute-start.18 = (f32[4,16,512]{2,1,0:T(8,128)S(1)}, f32[4,16,512]{2,1,0:T(8,128)S(1)}, u32[]{:S(2)}, u32[]{:S(2)}) collective-permute-start(f32[4,16,512]{2,1,0:T(8,128)S(1)} %get-tuple-element.32), channel_id=1, source_target_pairs={{2,1},{3,0},{4,3},{5,2},{6,5},{7,4},{10,9},{11,8},{12,11},{13,10},... | collective-permute-start | bytes 393224 | tf_op jit(solution)/shard_map/ppermute | solution.py:347
  (1 other events, 2.2 us)
